TPU v7x, 512 devices: a whole 4x4x16 slice. The times are simulated.
512 devices in a mesh: pos: 16 (over y, z_hi), ky: 4 (over z_lo), kz: 8 (over x, core).
Axes of the slice: x: 4, y: 4, z: 16 (z_hi: 4, z_lo: 4; z = z_hi * 4 + z_lo), core: 2. Of those that a mesh axis runs over, the one named last changes fastest.
Arguments:
- cotangent: float32 [64, 64, 128, 64], P('pos', 'ky', 'kz'), may hold values from -6 to 6
- start_state: float32 [64, 64, 128, 64], P('pos', 'ky', 'kz'), may hold values from 0.1 to 2
- section_state: float32 [64, 64, 128, 64], P('pos', 'ky', 'kz'), may hold values from 0.1 to 2
- face_codes: int32 [64, 64, 128, 64], P('pos', 'ky', 'kz'), may hold values from 0 to 1295
- field_strength: float32 [3, 64], P(None, 'pos'), may hold values from -4 to 4
- velocity: float32 [64, 128, 64], P('ky', 'kz'), may hold values from -4 to 4
- shell_index: int32 [64, 128, 64], P('ky', 'kz'), may hold values from 0 to 63
- shell_out: float32 [64, 128, 64], P('ky', 'kz'), may hold values from 0.5 to 2
- shell_in: float32 [64, 128, 64], P('ky', 'kz'), may hold values from 0.0055242716 to 0.022097087
Outputs:
- state_adjoint: float32 [64, 64, 128, 64], P('pos', 'ky', 'kz')
- field_grad: float32 [3, 64], P(None, 'pos')
Inputs may be any that keep to these rules, and one draw needn't show every extreme that they name: `face_codes`: each entry packs four digits of 0 to 5, one each for position, ky, kz, kx; the digit of dimension d is the entry divided by 6**d, modulo 6; digit // 3 is the upwind side and digit % 3 the reconstruction.
All inputs are finite; a program needn't handle non-finite values.
Results may differ from a plain program's by a relative error of at most 0.00011.
Values sent between devices are 32-bit elements; how exact they have to be, the bound alone decides.
No kernel may reach another device: no remote copies, remote signals or barrier semaphores. Data moves between devices by JAX's collectives and lax.ppermute only.
A program may use at most 64 MiB of HBM per device.

v0:
```python
import jax
import jax.numpy as jnp
from jax import lax
from jax.sharding import PartitionSpec as P

KX = 64
KY = 64
KZ = 128
SHELLS = 64


time_step = 0.25
RECONSTRUCTION = (
    (0.0, -0.5, 0.0, 0.0, 0.0, 0.0),
    (1.0, 1.5, 0.5, 0.0, 0.0, 0.5),
    (0.0, 0.0, 0.5, 1.0, 1.5, 0.5),
    (0.0, 0.0, 0.0, 0.0, -0.5, 0.0),
)


def shifted_2(array, axis, by):
    count = lax.axis_size(axis)
    pairs = [(i, i + by) for i in range(count) if 0 <= i + by < count]
    return lax.ppermute(array, axis, pairs)


def from_behind(value, axis, steps):
    count = lax.axis_size(axis)
    pairs = [(source, (source + steps) % count) for source in range(count)]
    return lax.ppermute(value, axis, pairs)


def padded_2(array, sides, width, wrap):
    for axis, dim in sides:
        count, length = (lax.axis_size(axis), array.shape[dim])
        up = [(i, (i + 1) % count) for i in range(count if wrap else count - 1)]
        down = [(j, i) for i, j in up]
        last = lax.slice_in_dim(array, length - width, length, axis=dim)
        first = lax.slice_in_dim(array, 0, width, axis=dim)
        before = lax.ppermute(last, axis, up)
        after = lax.ppermute(first, axis, down)
        array = jnp.concatenate([before, array, after], axis=dim)
    return array


def lookup(digits, values_table):
    summed = jnp.zeros(digits.shape, jnp.float32)
    for symbol in range(6):
        if values_table[symbol] != 0.0:
            summed = summed + jnp.where(
                digits == symbol, jnp.float32(values_table[symbol]), jnp.float32(0.0)
            )
    return summed


def coefficients(face_codes, digit_place):
    digits = face_codes // 6**digit_place % 6
    return [lookup(digits, weights_row) for weights_row in RECONSTRUCTION]


def differences(carried, following, along_dim):
    length = carried.shape[along_dim]
    shifted = jnp.concatenate(
        [lax.slice_in_dim(carried, 1, length, axis=along_dim), following], axis=along_dim
    )
    return carried - shifted


def rim_terms(differ, coeff_sets):
    low_side, centre, high_side, far_side = coeff_sets
    return jnp.stack([low_side * differ, high_side * differ, far_side * differ])


def finish(padded, differ, coeff_sets, along_dim, length):
    centre = coeff_sets[1]
    return (
        lax.slice_in_dim(padded[0], 3, 3 + length, axis=along_dim)
        + centre * differ
        + lax.slice_in_dim(padded[1], 1, 1 + length, axis=along_dim)
        + lax.slice_in_dim(padded[2], 0, length, axis=along_dim)
    )


def operator_adjoint(
    adjoint, field_strength, coeff_all, velocity, shell_table, shell_out, shell_in
):
    positions, rows_ky, rows_kz = (adjoint.shape[0], adjoint.shape[1], adjoint.shape[2])
    carried = velocity[None] * adjoint
    following = shifted_2(lax.slice_in_dim(carried, 0, 1, axis=0), "pos", -1)
    differ_pos = differences(carried, following, 0)
    next_ky = from_behind(lax.slice_in_dim(adjoint, 0, 1, axis=1), "ky", -1)
    next_kz = from_behind(lax.slice_in_dim(adjoint, 0, 1, axis=2), "kz", -1)
    differ_ky = differences(adjoint, next_ky, 1)
    differ_kz = differences(adjoint, next_kz, 2)
    padded_pos = padded_2(rim_terms(differ_pos, coeff_all[0]), (("pos", 1),), 2, False)
    across = finish(padded_pos, differ_pos, coeff_all[0], 0, positions)
    terms_ky = rim_terms(differ_ky, coeff_all[1])
    terms_kz = rim_terms(differ_kz, coeff_all[2])
    padded_ky = padded_2(terms_ky, (("ky", 2),), 2, True)
    padded_kz = padded_2(terms_kz, (("kz", 3),), 2, True)
    along_ky = finish(padded_ky, differ_ky, coeff_all[1], 1, rows_ky)
    along_kz = finish(padded_kz, differ_kz, coeff_all[2], 2, rows_kz)
    low_side, centre, high_side, far_side = coeff_all[3]
    differ_kx = adjoint - jnp.roll(adjoint, -1, 3)
    along_kx = (
        jnp.roll(low_side * differ_kx, -1, 3)
        + centre * differ_kx
        + jnp.roll(high_side * differ_kx, 1, 3)
        + jnp.roll(far_side * differ_kx, 2, 3)
    )
    momentum = (along_kx, along_ky, along_kz)
    weighted = (adjoint * shell_out[None]).reshape(positions, -1)
    local_totals = jnp.dot(
        weighted, shell_table, precision=lax.Precision.HIGHEST, preferred_element_type=jnp.float32
    )
    totals = lax.psum(local_totals, ("ky", "kz"))
    returned = jnp.dot(
        totals, shell_table.T, precision=lax.Precision.HIGHEST, preferred_element_type=jnp.float32
    )
    returned = returned.reshape(adjoint.shape) * shell_in[None]
    result = returned - across - adjoint
    for component in range(3):
        result = result - field_strength[component][:, None, None, None] * momentum[component]
    return (result, momentum)


def shards(
    cotangent,
    start_state,
    section_state,
    face_codes,
    field_strength,
    velocity,
    shell_index,
    shell_out,
    shell_in,
):
    coeff_all = [coefficients(face_codes, digit_place) for digit_place in range(4)]
    indices = shell_index.reshape(-1)
    shell_table = (indices[:, None] == jnp.arange(SHELLS, dtype=jnp.int32)[None, :]).astype(
        jnp.float32
    )
    applied, momentum = operator_adjoint(
        cotangent, field_strength, coeff_all, velocity, shell_table, shell_out, shell_in
    )
    section_adjoint = 0.5 * cotangent + 0.5 * time_step * applied
    local_grad = jnp.stack(
        [
            -0.5 * time_step * jnp.sum(section_state * momentum[component], axis=(1, 2, 3))
            for component in range(3)
        ]
    )
    applied, momentum = operator_adjoint(
        section_adjoint, field_strength, coeff_all, velocity, shell_table, shell_out, shell_in
    )
    state_adjoint = 0.5 * cotangent + section_adjoint + time_step * applied
    local_grad = local_grad - jnp.stack(
        [
            time_step * jnp.sum(start_state * momentum[component], axis=(1, 2, 3))
            for component in range(3)
        ]
    )
    normalizer = 1.0 / (KX * KY * KZ) ** 0.5
    field_grad = lax.psum(local_grad, ("ky", "kz")) * normalizer
    return (state_adjoint, field_grad)


def solution(mesh):
    return jax.shard_map(
        shards,
        mesh=mesh,
        in_specs=(
            P("pos", "ky", "kz", None),
            P("pos", "ky", "kz", None),
            P("pos", "ky", "kz", None),
            P("pos", "ky", "kz", None),
            P(None, "pos"),
            P("ky", "kz", None),
            P("ky", "kz", None),
            P("ky", "kz", None),
            P("ky", "kz", None),
        ),
        out_specs=(P("pos", "ky", "kz", None), P(None, "pos")),
        check_vma=False,
    )
```

profile of v0, /device:TPU:8, one launch (start us, length us, event | category | flops | bytes accessed | tf_op | source)
XLA Modules:
  0.0 400.7 jit_solution(13885034125317966116)
XLA Ops:
  1.8 2.2 collective-permute-start.6
  4.7 6.5 %collective-permute-start.3 = (f32[4,1,16,64]{3,2,1,0:T(8,128)S(1)}, f32[4,1,16,64]{3,2,1,0:T(8,128)S(1)}, u32[]{:S(2)}, u32[]{:S(2)}) collective-permute-start(f32[4,1,16,64]{3,2,1,0:T(8,128)S(1)} %slice.285), channel_id=1, source_target_pairs={{0,24},{8,0},{16,8},{24,16},{1,25},{9,1},{17,9},{25,17},{2,26},{10... | collective-permute-start | bytes 49160 | tf_op jit(solution)/shard_map/ppermute | solution.py:30
  16.9 4.4 %broadcast_multiply_fusion.3 = (f32[4,16,16,64]{3,2,1,0:T(8,128)}, f32[4,16,16,64]{3,2,1,0:T(8,128)S(1)}, f32[1,4,16,16,64]{4,3,2,1,0:T(8,128)S(1)}, f32[4,16,16...) fusion(f32[4,16,16,64]{3,2,1,0:T(8,128)S(1)} %copy-done.1, ...), kind=kLoop, calls=%fused_computation.186 | loop fusion | flops 3604480 | bytes 3538944 | tf_op jit(solution)/shard_map/mul | solution.py:112
  22.6 2.0 fusion.3
  24.5 68.0 %psum.21 = f32[4,64]{1,0:T(4,128)S(1)} all-reduce(f32[4,64]{1,0:T(4,128)S(1)} %fusion.3), channel_id=1, replica_groups=mesh['pos'=16,'ky'=4,'kz'=8] {'ky','kz'}, use_global_device_ids=true, to_apply=%region_0.1 | all-reduce | flops 256 | bytes 2048 | tf_op jit(solution)/shard_map/psum | solution.py:116
  93.2 10.3 %collective-permute-start = (f32[1,16,16,64]{3,2,1,0:T(8,128)}, f32[1,16,16,64]{3,2,1,0:T(8,128)}, u32[]{:S(2)}, u32[]{:S(2)}) collective-permute-start(f32[1,16,16,64]{3,2,1,0:T(8,128)} %slice.344), channel_id=1, source_target_pairs={{32,0},{64,32},{96,64},{128,96},{160,128},{192,160},{224,192},{256... | collective-permute-start | bytes 196616 | tf_op jit(solution)/shard_map/ppermute | solution.py:24
  103.5 2.1 fusion.2
  105.6 2.0 reshape.84
  109.3 2.9 multiply_bitcast_fusion.5
  112.4 2.9 collective-permute-start.8
  117.3 5.7 %collective-permute-start.5 = (f32[3,4,2,16,64]{4,3,2,1,0:T(8,128)S(1)}, f32[3,4,2,16,64]{4,3,2,1,0:T(8,128)S(1)}, u32[]{:S(2)}, u32[]{:S(2)}) collective-permute-start(f32[3,4,2,16,64]{4,3,2,1,0:T(8,128)S(1)} %get-tuple-element.57), channel_id=1, source_target_pairs={{8,0},{16,8},{24,16},{0,24},{9,1},{17,9},{25,17},{1,25},{10,2},{18... | collective-permute-start | bytes 294920 | tf_op jit(solution)/shard_map/ppermute | solution.py:41
  123.7 7.5 %collective-permute-start.1 = (f32[3,2,16,16,64]{4,3,2,1,0:T(8,128)S(1)}, f32[3,2,16,16,64]{4,3,2,1,0:T(8,128)S(1)}, u32[]{:S(2)}, u32[]{:S(2)}) collective-permute-start(f32[3,2,16,16,64]{4,3,2,1,0:T(8,128)S(1)} %get-tuple-element.52), channel_id=1, source_target_pairs={{32,0},{64,32},{96,64},{128,96},{160,128},{192,160},{224,192},{256... | collective-permute-start | bytes 1179656 | tf_op jit(solution)/shard_map/ppermute | solution.py:41
  131.2 2.3 collective-permute-start.2
  134.2 21.6 %collective-permute-done.4 = f32[3,4,2,16,64]{4,3,2,1,0:T(8,128)S(1)} collective-permute-done((f32[3,4,2,16,64]{4,3,2,1,0:T(8,128)S(1)}, f32[3,4,2,16,64]{4,3,2,1,0:T(8,128)S(1)}, u32[]{:S(2)}, u32[]{:S(2)}) %collective-permute-start.4) | collective-permute-done | bytes 98336 | tf_op jit(solution)/shard_map/ppermute | solution.py:40
  155.8 8.8 %collective-permute-done.5 = f32[3,4,2,16,64]{4,3,2,1,0:T(8,128)S(1)} collective-permute-done((f32[3,4,2,16,64]{4,3,2,1,0:T(8,128)S(1)}, f32[3,4,2,16,64]{4,3,2,1,0:T(8,128)S(1)}, u32[]{:S(2)}, u32[]{:S(2)}) %collective-permute-start.5) | collective-permute-done | bytes 98336 | tf_op jit(solution)/shard_map/ppermute | solution.py:41
  165.8 3.4 multiply_reduce_fusion.5
  169.2 28.9 %collective-permute-done.2 = f32[3,2,16,16,64]{4,3,2,1,0:T(8,128)S(1)} collective-permute-done((f32[3,2,16,16,64]{4,3,2,1,0:T(8,128)S(1)}, f32[3,2,16,16,64]{4,3,2,1,0:T(8,128)S(1)}, u32[]{:S(2)}, u32[]{:S(2)}) %collective-permute-start.2) | collective-permute-done | bytes 393248 | tf_op jit(solution)/shard_map/ppermute | solution.py:40
  199.1 2.1 collective-permute-start.12
  204.9 3.2 fusion.20
  208.1 3.8 collective-permute-start.9
  212.0 2.0 fusion.1
  214.2 12.1 %collective-permute-done.9 = f32[1,16,16,64]{3,2,1,0:T(8,128)S(1)} collective-permute-done((f32[1,16,16,64]{3,2,1,0:T(8,128)S(1)}, f32[1,16,16,64]{3,2,1,0:T(8,128)S(1)}, u32[]{:S(2)}, u32[]{:S(2)}) %collective-permute-start.9) | collective-permute-done | bytes 65568 | tf_op jit(solution)/shard_map/ppermute | solution.py:24
  226.3 2.7 multiply_bitcast_fusion
  229.2 2.9 collective-permute-start.17
  232.2 1.9 collective-permute-start.13
  234.1 5.7 %collective-permute-start.14 = (f32[3,4,2,16,64]{4,3,2,1,0:T(8,128)S(1)}, f32[3,4,2,16,64]{4,3,2,1,0:T(8,128)S(1)}, u32[]{:S(2)}, u32[]{:S(2)}) collective-permute-start(f32[3,4,2,16,64]{4,3,2,1,0:T(8,128)S(1)} %get-tuple-element.49), channel_id=1, source_target_pairs={{8,0},{16,8},{24,16},{0,24},{9,1},{17,9},{25,17},{1,25},{10,2},{18... | collective-permute-start | bytes 294920 | tf_op jit(solution)/shard_map/ppermute | solution.py:41
  245.8 4.3 %multiply_reduce_fusion.2 = (f32[4]{0:T(128)S(1)}, f32[4]{0:T(128)S(1)}, f32[4]{0:T(128)S(1)}, f32[4,16,16,64]{3,2,1,0:T(8,128)}, f32[4,16,16,64]{3,2,1,0:T(8,12...) fusion(f32[4,16,16,64]{3,2,1,0:T(8,128)S(1)} %copy-done.9, ...), kind=kLoop, calls=%fused_computation.151 | loop fusion | flops 7208948 | bytes 5242928 | tf_op jit(solution)/shard_map/reduce_sum | solution.py:159
  251.6 4.6 %collective-permute-start.10 = (f32[3,2,16,16,64]{4,3,2,1,0:T(8,128)}, f32[3,2,16,16,64]{4,3,2,1,0:T(8,128)}, u32[]{:S(2)}, u32[]{:S(2)}) collective-permute-start(f32[3,2,16,16,64]{4,3,2,1,0:T(8,128)} %get-tuple-element.50), channel_id=1, source_target_pairs={{32,0},{64,32},{96,64},{128,96},{160,128},{192,160},{224,192},{256... | collective-permute-start | bytes 1179656 | tf_op jit(solution)/shard_map/ppermute | solution.py:41
  256.2 5.2 %collective-permute-start.11 = (f32[3,2,16,16,64]{4,3,2,1,0:T(8,128)}, f32[3,2,16,16,64]{4,3,2,1,0:T(8,128)}, u32[]{:S(2)}, u32[]{:S(2)}) collective-permute-start(f32[3,2,16,16,64]{4,3,2,1,0:T(8,128)} %get-tuple-element.51), channel_id=1, source_target_pairs={{0,32},{32,64},{64,96},{96,128},{128,160},{160,192},{192,224},{224... | collective-permute-start | bytes 1179656 | tf_op jit(solution)/shard_map/ppermute | solution.py:40
  261.5 131.9 %all-reduce = (f32[4,64]{1,0:T(4,128)}, f32[3,4]{1,0:T(4,128)S(1)}) all-reduce(f32[4,64]{1,0:T(4,128)S(1)} %fusion.1, f32[3,4]{1,0:T(4,128)S(1)} %maximum_subtract_fusion.8), channel_id=1, replica_groups=mesh['pos'=16,'ky'=4,'kz'=8] {'ky','kz'}, use_global_device_ids=true, to_apply=%region_1.2 | all-reduce | flops 268 | bytes 2144 | tf_op jit(solution)/shard_map/psum | solution.py:116
  393.3 2.2 fusion
  397.3 3.4 fusion.35
  (106 shorter events, 29.9 us)
Async XLA Ops:
  0.6 15.1 %copy-start.1 = (f32[4,16,16,64]{3,2,1,0:T(8,128)S(1)}, f32[4,16,16,64]{3,2,1,0:T(8,128)}, u32[]{:S(2)}) copy-start(f32[4,16,16,64]{3,2,1,0:T(8,128)} %param.9) | copy-start | bytes 786436
  0.6 16.1 %copy-start.15 = (s32[16,16,64]{2,1,0:T(8,128)S(1)}, s32[16,16,64]{2,1,0:T(8,128)}, u32[]{:S(2)}) copy-start(s32[16,16,64]{2,1,0:T(8,128)} %param.15) | copy-start | bytes 196612
  0.7 16.2 %copy-start = (s32[4,16,16,64]{3,2,1,0:T(8,128)S(1)}, s32[4,16,16,64]{3,2,1,0:T(8,128)}, u32[]{:S(2)}) copy-start(s32[4,16,16,64]{3,2,1,0:T(8,128)} %param.12) | copy-start | bytes 786436
  0.7 16.2 %copy-start.10 = (f32[16,16,64]{2,1,0:T(8,128)S(1)}, f32[16,16,64]{2,1,0:T(8,128)}, u32[]{:S(2)}) copy-start(f32[16,16,64]{2,1,0:T(8,128)} %param.16) | copy-start | bytes 196612
  0.7 16.2 %copy-start.12 = (f32[16,16,64]{2,1,0:T(8,128)S(1)}, f32[16,16,64]{2,1,0:T(8,128)}, u32[]{:S(2)}) copy-start(f32[16,16,64]{2,1,0:T(8,128)} %param.14) | copy-start | bytes 196612
  1.8 15.1 %collective-permute-start.6 = (f32[4,16,1,64]{3,2,1,0:T(1,128)S(1)}, f32[4,16,1,64]{3,2,1,0:T(1,128)S(1)}, u32[]{:S(2)}, u32[]{:S(2)}) collective-permute-start(f32[4,16,1,64]{3,2,1,0:T(1,128)S(1)} %slice.296), channel_id=1, source_target_pairs={{0,7},{1,0},{2,1},{3,2},{4,3},{5,4},{6,5},{7,6},{8,15},{9,8},{10,9... | collective-permute-start | bytes 49160 | tf_op jit(solution)/shard_map/ppermute | solution.py:30
  4.7 12.2 %collective-permute-start.3 = (f32[4,1,16,64]{3,2,1,0:T(8,128)S(1)}, f32[4,1,16,64]{3,2,1,0:T(8,128)S(1)}, u32[]{:S(2)}, u32[]{:S(2)}) collective-permute-start(f32[4,1,16,64]{3,2,1,0:T(8,128)S(1)} %slice.285), channel_id=1, source_target_pairs={{0,24},{8,0},{16,8},{24,16},{1,25},{9,1},{17,9},{25,17},{2,26},{10... | collective-permute-start | bytes 49160 | tf_op jit(solution)/shard_map/ppermute | solution.py:30
  16.9 86.7 %copy-start.16 = (s32[16384]{0:T(1024)}, s32[16384]{0:T(1024)S(1)}, u32[]{:S(2)}) copy-start(s32[16384]{0:T(1024)S(1)} %eq.108) | copy-start | bytes 196612
  93.2 14.7 %collective-permute-start = (f32[1,16,16,64]{3,2,1,0:T(8,128)}, f32[1,16,16,64]{3,2,1,0:T(8,128)}, u32[]{:S(2)}, u32[]{:S(2)}) collective-permute-start(f32[1,16,16,64]{3,2,1,0:T(8,128)} %slice.344), channel_id=1, source_target_pairs={{32,0},{64,32},{96,64},{128,96},{160,128},{192,160},{224,192},{256... | collective-permute-start | bytes 196616 | tf_op jit(solution)/shard_map/ppermute | solution.py:24
  112.4 18.8 %collective-permute-start.7 = (f32[3,4,16,2,64]{4,3,2,1,0:T(2,128)S(1)}, f32[3,4,16,2,64]{4,3,2,1,0:T(2,128)S(1)}, u32[]{:S(2)}, u32[]{:S(2)}) collective-permute-start(f32[3,4,16,2,64]{4,3,2,1,0:T(2,128)S(1)} %get-tuple-element.54), channel_id=1, source_target_pairs={{0,1},{1,2},{2,3},{3,4},{4,5},{5,6},{6,7},{7,0},{8,9},{9,10},{10,1... | collective-permute-start | bytes 294920 | tf_op jit(solution)/shard_map/ppermute | solution.py:40
  112.4 21.1 %collective-permute-start.8 = (f32[3,4,16,2,64]{4,3,2,1,0:T(2,128)S(1)}, f32[3,4,16,2,64]{4,3,2,1,0:T(2,128)S(1)}, u32[]{:S(2)}, u32[]{:S(2)}) collective-permute-start(f32[3,4,16,2,64]{4,3,2,1,0:T(2,128)S(1)} %get-tuple-element.55), channel_id=1, source_target_pairs={{1,0},{2,1},{3,2},{4,3},{5,4},{6,5},{7,6},{0,7},{9,8},{10,9},{11,1... | collective-permute-start | bytes 294920 | tf_op jit(solution)/shard_map/ppermute | solution.py:41
  115.4 40.3 %collective-permute-start.4 = (f32[3,4,2,16,64]{4,3,2,1,0:T(8,128)S(1)}, f32[3,4,2,16,64]{4,3,2,1,0:T(8,128)S(1)}, u32[]{:S(2)}, u32[]{:S(2)}) collective-permute-start(f32[3,4,2,16,64]{4,3,2,1,0:T(8,128)S(1)} %get-tuple-element.56), channel_id=1, source_target_pairs={{0,8},{8,16},{16,24},{24,0},{1,9},{9,17},{17,25},{25,1},{2,10},{10... | collective-permute-start | bytes 294920 | tf_op jit(solution)/shard_map/ppermute | solution.py:40
  117.3 47.2 %collective-permute-start.5 = (f32[3,4,2,16,64]{4,3,2,1,0:T(8,128)S(1)}, f32[3,4,2,16,64]{4,3,2,1,0:T(8,128)S(1)}, u32[]{:S(2)}, u32[]{:S(2)}) collective-permute-start(f32[3,4,2,16,64]{4,3,2,1,0:T(8,128)S(1)} %get-tuple-element.57), channel_id=1, source_target_pairs={{8,0},{16,8},{24,16},{0,24},{9,1},{17,9},{25,17},{1,25},{10,2},{18... | collective-permute-start | bytes 294920 | tf_op jit(solution)/shard_map/ppermute | solution.py:41
  123.7 45.5 %collective-permute-start.1 = (f32[3,2,16,16,64]{4,3,2,1,0:T(8,128)S(1)}, f32[3,2,16,16,64]{4,3,2,1,0:T(8,128)S(1)}, u32[]{:S(2)}, u32[]{:S(2)}) collective-permute-start(f32[3,2,16,16,64]{4,3,2,1,0:T(8,128)S(1)} %get-tuple-element.52), channel_id=1, source_target_pairs={{32,0},{64,32},{96,64},{128,96},{160,128},{192,160},{224,192},{256... | collective-permute-start | bytes 1179656 | tf_op jit(solution)/shard_map/ppermute | solution.py:41
  131.2 66.9 %collective-permute-start.2 = (f32[3,2,16,16,64]{4,3,2,1,0:T(8,128)S(1)}, f32[3,2,16,16,64]{4,3,2,1,0:T(8,128)S(1)}, u32[]{:S(2)}, u32[]{:S(2)}) collective-permute-start(f32[3,2,16,16,64]{4,3,2,1,0:T(8,128)S(1)} %get-tuple-element.53), channel_id=1, source_target_pairs={{0,32},{32,64},{64,96},{96,128},{128,160},{160,192},{192,224},{224... | collective-permute-start | bytes 1179656 | tf_op jit(solution)/shard_map/ppermute | solution.py:40
  165.8 32.3 %copy-start.6 = (f32[4,16,16,64]{3,2,1,0:T(8,128)S(1)}, f32[4,16,16,64]{3,2,1,0:T(8,128)}, u32[]{:S(2)}) copy-start(f32[4,16,16,64]{3,2,1,0:T(8,128)} %reshape.84) | copy-start | bytes 786436
  165.8 32.3 %copy-start.7 = (f32[16,16,64]{2,1,0:T(8,128)S(1)}, f32[16,16,64]{2,1,0:T(8,128)}, u32[]{:S(2)}) copy-start(f32[16,16,64]{2,1,0:T(8,128)} %param.17) | copy-start | bytes 196612
  165.8 32.3 %copy-start.11 = (f32[16,16,64]{2,1,0:T(8,128)S(1)}, f32[16,16,64]{2,1,0:T(8,128)}, u32[]{:S(2)}) copy-start(f32[16,16,64]{2,1,0:T(8,128)} %param.16) | copy-start | bytes 196612
  199.0 5.9 %copy-start.13 = (f32[16,16,64]{2,1,0:T(8,128)S(1)}, f32[16,16,64]{2,1,0:T(8,128)}, u32[]{:S(2)}) copy-start(f32[16,16,64]{2,1,0:T(8,128)} %param.14) | copy-start | bytes 196612
  199.0 4.6 %collective-permute-start.15 = (f32[4,16,1,64]{3,2,1,0:T(1,128)S(1)}, f32[4,16,1,64]{3,2,1,0:T(1,128)S(1)}, u32[]{:S(2)}, u32[]{:S(2)}) collective-permute-start(f32[4,16,1,64]{3,2,1,0:T(1,128)S(1)} %slice.386), channel_id=1, source_target_pairs={{0,7},{1,0},{2,1},{3,2},{4,3},{5,4},{6,5},{7,6},{8,15},{9,8},{10,9... | collective-permute-start | bytes 49160 | tf_op jit(solution)/shard_map/ppermute | solution.py:30
  199.1 5.8 %collective-permute-start.12 = (f32[4,1,16,64]{3,2,1,0:T(8,128)S(1)}, f32[4,1,16,64]{3,2,1,0:T(8,128)S(1)}, u32[]{:S(2)}, u32[]{:S(2)}) collective-permute-start(f32[4,1,16,64]{3,2,1,0:T(8,128)S(1)} %slice.378), channel_id=1, source_target_pairs={{0,24},{8,0},{16,8},{24,16},{1,25},{9,1},{17,9},{25,17},{2,26},{10... | collective-permute-start | bytes 49160 | tf_op jit(solution)/shard_map/ppermute | solution.py:30
  204.9 7.1 %copy-start.14 = (f32[4,16384]{1,0:T(4,128)S(1)}, f32[4,16384]{1,0:T(4,128)}, u32[]{:S(2)}) copy-start(f32[4,16384]{1,0:T(4,128)} %reshape.85) | copy-start | bytes 786436
  204.9 7.1 %copy-start.17 = (s32[16384]{0:T(1024)S(1)}, s32[16384]{0:T(1024)}, u32[]{:S(2)}) copy-start(s32[16384]{0:T(1024)} %copy-done.16) | copy-start | bytes 196612
  208.1 18.1 %collective-permute-start.9 = (f32[1,16,16,64]{3,2,1,0:T(8,128)S(1)}, f32[1,16,16,64]{3,2,1,0:T(8,128)S(1)}, u32[]{:S(2)}, u32[]{:S(2)}) collective-permute-start(f32[1,16,16,64]{3,2,1,0:T(8,128)S(1)} %slice.366), channel_id=1, source_target_pairs={{32,0},{64,32},{96,64},{128,96},{160,128},{192,160},{224,192},{256... | collective-permute-start | bytes 196616 | tf_op jit(solution)/shard_map/ppermute | solution.py:24
  229.2 11.1 %collective-permute-start.16 = (f32[3,4,16,2,64]{4,3,2,1,0:T(2,128)S(1)}, f32[3,4,16,2,64]{4,3,2,1,0:T(2,128)S(1)}, u32[]{:S(2)}, u32[]{:S(2)}) collective-permute-start(f32[3,4,16,2,64]{4,3,2,1,0:T(2,128)S(1)} %get-tuple-element.46), channel_id=1, source_target_pairs={{0,1},{1,2},{2,3},{3,4},{4,5},{5,6},{6,7},{7,0},{8,9},{9,10},{10,1... | collective-permute-start | bytes 294920 | tf_op jit(solution)/shard_map/ppermute | solution.py:40
  229.2 11.1 %collective-permute-start.17 = (f32[3,4,16,2,64]{4,3,2,1,0:T(2,128)S(1)}, f32[3,4,16,2,64]{4,3,2,1,0:T(2,128)S(1)}, u32[]{:S(2)}, u32[]{:S(2)}) collective-permute-start(f32[3,4,16,2,64]{4,3,2,1,0:T(2,128)S(1)} %get-tuple-element.47), channel_id=1, source_target_pairs={{1,0},{2,1},{3,2},{4,3},{5,4},{6,5},{7,6},{0,7},{9,8},{10,9},{11,1... | collective-permute-start | bytes 294920 | tf_op jit(solution)/shard_map/ppermute | solution.py:41
  232.2 10.5 %collective-permute-start.13 = (f32[3,4,2,16,64]{4,3,2,1,0:T(8,128)S(1)}, f32[3,4,2,16,64]{4,3,2,1,0:T(8,128)S(1)}, u32[]{:S(2)}, u32[]{:S(2)}) collective-permute-start(f32[3,4,2,16,64]{4,3,2,1,0:T(8,128)S(1)} %get-tuple-element.48), channel_id=1, source_target_pairs={{0,8},{8,16},{16,24},{24,0},{1,9},{9,17},{17,25},{25,1},{2,10},{10... | collective-permute-start | bytes 294920 | tf_op jit(solution)/shard_map/ppermute | solution.py:40
  234.1 10.4 %collective-permute-start.14 = (f32[3,4,2,16,64]{4,3,2,1,0:T(8,128)S(1)}, f32[3,4,2,16,64]{4,3,2,1,0:T(8,128)S(1)}, u32[]{:S(2)}, u32[]{:S(2)}) collective-permute-start(f32[3,4,2,16,64]{4,3,2,1,0:T(8,128)S(1)} %get-tuple-element.49), channel_id=1, source_target_pairs={{8,0},{16,8},{24,16},{0,24},{9,1},{17,9},{25,17},{1,25},{10,2},{18... | collective-permute-start | bytes 294920 | tf_op jit(solution)/shard_map/ppermute | solution.py:41
  250.3 11.2 %copy-start.18 = (f32[1,4]{1,0:T(1,128)S(1)}, f32[1,4]{1,0:T(1,128)}, u32[]{:S(2)}) copy-start(f32[1,4]{1,0:T(1,128)} %get-tuple-element.108) | copy-start | bytes 52
  250.3 11.2 %copy-start.19 = (f32[1,4]{1,0:T(1,128)S(1)}, f32[1,4]{1,0:T(1,128)}, u32[]{:S(2)}) copy-start(f32[1,4]{1,0:T(1,128)} %get-tuple-element.109) | copy-start | bytes 52
  251.6 145.6 %collective-permute-start.10 = (f32[3,2,16,16,64]{4,3,2,1,0:T(8,128)}, f32[3,2,16,16,64]{4,3,2,1,0:T(8,128)}, u32[]{:S(2)}, u32[]{:S(2)}) collective-permute-start(f32[3,2,16,16,64]{4,3,2,1,0:T(8,128)} %get-tuple-element.50), channel_id=1, source_target_pairs={{32,0},{64,32},{96,64},{128,96},{160,128},{192,160},{224,192},{256... | collective-permute-start | bytes 1179656 | tf_op jit(solution)/shard_map/ppermute | solution.py:41
  256.2 141.0 %collective-permute-start.11 = (f32[3,2,16,16,64]{4,3,2,1,0:T(8,128)}, f32[3,2,16,16,64]{4,3,2,1,0:T(8,128)}, u32[]{:S(2)}, u32[]{:S(2)}) collective-permute-start(f32[3,2,16,16,64]{4,3,2,1,0:T(8,128)} %get-tuple-element.51), channel_id=1, source_target_pairs={{0,32},{32,64},{64,96},{96,128},{128,160},{160,192},{192,224},{224... | collective-permute-start | bytes 1179656 | tf_op jit(solution)/shard_map/ppermute | solution.py:40
  (6 other events, 8.4 us)
where the time goes:
time: 402 us; the launch traced here: 401 us
  blocking collectives  200 us (50%)
  waiting for transfers between devices  76.1 us (19%)
  starting transfers between devices  65.7 us (16%)
  other arithmetic  29.9 us (7%)
  local copies, waits for them, and re-layouts  19.7 us (5%)
  matrix products  8.28 us (2%)
    psum x2, blocking collectives, operator_adjoint(): totals = lax.psum(local_totals, ('ky', 'kz'))  200 us
    ppermute x6, waiting for transfers between devices, padded_2(): before = lax.ppermute(last, axis, up)  52.2 us
    ppermute x6, starting transfers between devices, padded_2(): after = lax.ppermute(first, axis, down)  29.4 us
    ppermute x2, starting transfers between devices, shifted_2(): return lax.ppermute(array, axis, pairs)  14.1 us
    ppermute x2, waiting for transfers between devices, shifted_2(): return lax.ppermute(array, axis, pairs)  12.1 us
    ppermute x6, starting transfers between devices, padded_2(): before = lax.ppermute(last, axis, up)  11.3 us
    ppermute x4, starting transfers between devices, from_behind(): return lax.ppermute(value, axis, pairs)  10.8 us
    ppermute x6, waiting for transfers between devices, padded_2(): after = lax.ppermute(first, axis, down)  10.6 us
  transfers between devices with their start and end apart: 18, of which 7 were waited for; matrix products, arithmetic and copies ran while one was open for 6% of the time, Pallas kernels for 0%

commit v1 on v0

--- a/solution.py
+++ b/solution.py
@@ -41,6 +41,12 @@
         after = lax.ppermute(first, axis, down)
         array = jnp.concatenate([before, array, after], axis=dim)
     return array
+
+
+def sum_over_momentum(value):
+    count = lax.axis_size("ky") * lax.axis_size("kz")
+    copies = jnp.broadcast_to(value[None], (count,) + value.shape)
+    return jnp.sum(lax.all_to_all(copies, ("ky", "kz"), 0, 0), axis=0)
 
 
 def lookup(digits, values_table):
@@ -113,7 +119,7 @@
     local_totals = jnp.dot(
         weighted, shell_table, precision=lax.Precision.HIGHEST, preferred_element_type=jnp.float32
     )
-    totals = lax.psum(local_totals, ("ky", "kz"))
+    totals = sum_over_momentum(local_totals)
     returned = jnp.dot(
         totals, shell_table.T, precision=lax.Precision.HIGHEST, preferred_element_type=jnp.float32
     )
@@ -161,7 +167,7 @@
         ]
     )
     normalizer = 1.0 / (KX * KY * KZ) ** 0.5
-    field_grad = lax.psum(local_grad, ("ky", "kz")) * normalizer
+    field_grad = sum_over_momentum(local_grad) * normalizer
     return (state_adjoint, field_grad)
 
 

time: 402 us -> 317 us (0.79)
  the two profiles are of different devices: /device:TPU:8 before, /device:TPU:18 now
where the time goes in v1:
time: 317 us; the launch traced here: 315 us
  waiting for transfers between devices  127 us (40%)
  starting transfers between devices  80.1 us (25%)
  other arithmetic  48.7 us (15%)
  local copies, waits for them, and re-layouts  30.1 us (9%)
  matrix products  27.9 us (9%)
    ppermute x6, waiting for transfers between devices, padded_2(): after = lax.ppermute(first, axis, down)  94.2 us
    ppermute x6, starting transfers between devices, padded_2(): after = lax.ppermute(first, axis, down)  27.5 us
    dot_general x2, matrix products, operator_adjoint(): jnp.dot(totals, shell_table.T, precision=lax.Precision.HIGHEST, preferred...  23.9 us
    ppermute x6, waiting for transfers between devices, padded_2(): before = lax.ppermute(last, axis, up)  21.6 us
    all_to_all x3, starting transfers between devices, sum_over_momentum(): return jnp.sum(lax.all_to_all(copies, ('ky', 'kz'), 0, 0), axis=0)  19.9 us
    another operation x6, other arithmetic, rim_terms(): return jnp.stack([low_side * differ, high_side * differ, far_side * differ])  16.4 us
    ppermute x2, starting transfers between devices, shifted_2(): return lax.ppermute(array, axis, pairs)  12.7 us
    ppermute x6, starting transfers between devices, padded_2(): before = lax.ppermute(last, axis, up)  10.9 us
  transfers between devices with their start and end apart: 21, of which 6 were waited for; matrix products, arithmetic and copies ran while one was open for 25% of the time, Pallas kernels for 0%

profile of v1, /device:TPU:18, one launch (start us, length us, event | category | flops | bytes accessed | tf_op | source)
XLA Modules:
  0.0 315.1 jit_solution(11657408795435036967)
XLA Ops:
  2.6 6.5 %collective-permute-start.3 = (f32[4,1,16,64]{3,2,1,0:T(8,128)S(1)}, f32[4,1,16,64]{3,2,1,0:T(8,128)S(1)}, u32[]{:S(2)}, u32[]{:S(2)}) collective-permute-start(f32[4,1,16,64]{3,2,1,0:T(8,128)S(1)} %slice.285), channel_id=1, source_target_pairs={{0,24},{8,0},{16,8},{24,16},{1,25},{9,1},{17,9},{25,17},{2,26},{10... | collective-permute-start | bytes 49160 | tf_op jit(solution)/shard_map/ppermute | solution.py:30
  13.2 4.4 %broadcast_multiply_fusion.3 = (f32[4,16,16,64]{3,2,1,0:T(8,128)}, f32[4,16,16,64]{3,2,1,0:T(8,128)S(1)}, f32[1,4,16,16,64]{4,3,2,1,0:T(8,128)}, f32[4,16,16,64]...) fusion(f32[4,16,16,64]{3,2,1,0:T(8,128)S(1)} %copy-done.1, ...), kind=kLoop, calls=%fused_computation.189 | loop fusion | flops 3604480 | bytes 3538944 | tf_op jit(solution)/shard_map/mul | solution.py:118
  19.0 9.9 %collective-permute-start = (f32[1,16,16,64]{3,2,1,0:T(8,128)S(1)}, f32[1,16,16,64]{3,2,1,0:T(8,128)}, u32[]{:S(2)}, u32[]{:S(2)}) collective-permute-start(f32[1,16,16,64]{3,2,1,0:T(8,128)S(1)} %slice.344), channel_id=1, source_target_pairs={{32,0},{64,32},{96,64},{128,96},{160,128},{192,160},{224,192},{256... | collective-permute-start | bytes 196616 | tf_op jit(solution)/shard_map/ppermute | solution.py:24
  29.0 2.0 fusion.5
  31.8 6.7 %all-to-all-start = ((f32[32,1,256]{2,1,0:T(1,128)}), f32[32,1,256]{2,1,0:T(1,128)}, u32[]{:S(2)}, u32[]{:S(2)}) async-start(f32[32,1,256]{2,1,0:T(1,128)} %reshape.146), calls=%async_computation | async-start | bytes 65536 | tf_op jit(solution)/shard_map/all_to_all | solution.py:49
  40.8 4.3 %multiply_bitcast_fusion.5 = (f32[1,4,16,16,64]{4,3,2,1,0:T(8,128)S(1)}, f32[1,4,16,16,64]{4,3,2,1,0:T(8,128)S(1)}, f32[1,4,16,16,64]{4,3,2,1,0:T(8,128)S(1)}, f...) fusion(f32[4,16,16,64]{3,2,1,0:T(8,128)S(1)} %get-tuple-element, ...), kind=kLoop, calls=%fused_computation.166 | loop fusion | flops 6488064 | bytes 3407872 | tf_op jit(solution)/shard_map/stack | solution.py:77
  48.7 3.4 %collective-permute-start.4 = (f32[3,4,2,16,64]{4,3,2,1,0:T(8,128)}, f32[3,4,2,16,64]{4,3,2,1,0:T(8,128)}, u32[]{:S(2)}, u32[]{:S(2)}) collective-permute-start(f32[3,4,2,16,64]{4,3,2,1,0:T(8,128)} %get-tuple-element.62), channel_id=1, source_target_pairs={{0,8},{8,16},{16,24},{24,0},{1,9},{9,17},{17,25},{25,1},{2,10},{10... | collective-permute-start | bytes 294920 | tf_op jit(solution)/shard_map/ppermute | solution.py:40
  52.1 4.2 %collective-permute-start.5 = (f32[3,4,2,16,64]{4,3,2,1,0:T(8,128)}, f32[3,4,2,16,64]{4,3,2,1,0:T(8,128)}, u32[]{:S(2)}, u32[]{:S(2)}) collective-permute-start(f32[3,4,2,16,64]{4,3,2,1,0:T(8,128)} %get-tuple-element.63), channel_id=1, source_target_pairs={{8,0},{16,8},{24,16},{0,24},{9,1},{17,9},{25,17},{1,25},{10,2},{18... | collective-permute-start | bytes 294920 | tf_op jit(solution)/shard_map/ppermute | solution.py:41
  59.9 6.8 %collective-permute-start.1 = (f32[3,2,16,16,64]{4,3,2,1,0:T(8,128)}, f32[3,2,16,16,64]{4,3,2,1,0:T(8,128)}, u32[]{:S(2)}, u32[]{:S(2)}) collective-permute-start(f32[3,2,16,16,64]{4,3,2,1,0:T(8,128)} %get-tuple-element.58), channel_id=1, source_target_pairs={{32,0},{64,32},{96,64},{128,96},{160,128},{192,160},{224,192},{256... | collective-permute-start | bytes 1179656 | tf_op jit(solution)/shard_map/ppermute | solution.py:41
  68.9 12.1 %fusion.1 = f32[4,16,16,64]{3,0,2,1:T(4,128)S(1)} fusion(s32[16,16,64]{2,1,0:T(8,128)} %param.15, f32[4,64]{1,0:T(4,128)S(1)} %reduce_sum.81), kind=kOutput, calls=%fused_computation.2 | convolution fusion | flops 51380224 | bytes 328704 | tf_op jit(solution)/shard_map/dot_general | solution.py:123
  81.0 3.0 collective-permute-start.2
  90.1 3.4 %multiply_reduce_fusion.5 = (f32[4]{0:T(128)S(1)}, f32[4]{0:T(128)S(1)}, f32[4]{0:T(128)S(1)}, f32[4,16,16,64]{3,2,1,0:T(8,128)S(1)}, f32[4,16,16,64]{3,2,1,0:T(8,128)S(1)}, /*index=5*/f32[4,16,16,64]{3,2,1,0:T(8,128)S(1)}) fusion(f32[4,16,16,64]{3,2,1,0:T(8,128)S(1)} %copy-done.51, f32[4,16,16,62]{3,2,1,0:T(8,128)S(1)} %bitcast.172, ...), kind=kLoop, calls=%fused_computation.157 | loop fusion | flops 6029300 | bytes 4456496 | tf_op jit(solution)/shard_map/reduce_sum | solution.py:155
  93.6 41.8 %collective-permute-done.1 = f32[3,2,16,16,64]{4,3,2,1,0:T(8,128)} collective-permute-done((f32[3,2,16,16,64]{4,3,2,1,0:T(8,128)}, f32[3,2,16,16,64]{4,3,2,1,0:T(8,128)}, u32[]{:S(2)}, u32[]{:S(2)}) %collective-permute-start.1) | collective-permute-done | bytes 393248 | tf_op jit(solution)/shard_map/ppermute | solution.py:41
  135.4 11.8 %collective-permute-done.2 = f32[3,2,16,16,64]{4,3,2,1,0:T(8,128)S(1)} collective-permute-done((f32[3,2,16,16,64]{4,3,2,1,0:T(8,128)S(1)}, f32[3,2,16,16,64]{4,3,2,1,0:T(8,128)S(1)}, u32[]{:S(2)}, u32[]{:S(2)}) %collective-permute-start.2) | collective-permute-done | bytes 393248 | tf_op jit(solution)/shard_map/ppermute | solution.py:40
  149.4 2.1 collective-permute-start.12
  155.7 8.5 %collective-permute-done.12 = f32[4,1,16,64]{3,2,1,0:T(8,128)S(1)} collective-permute-done((f32[4,1,16,64]{3,2,1,0:T(8,128)S(1)}, f32[4,1,16,64]{3,2,1,0:T(8,128)S(1)}, u32[]{:S(2)}, u32[]{:S(2)}) %collective-permute-start.12) | collective-permute-done | bytes 16416 | tf_op jit(solution)/shard_map/ppermute | solution.py:30
  164.2 4.5 %fusion.20 = (f32[1,4,16,16,64]{4,3,2,1,0:T(8,128)}, f32[4,16,16,64]{3,2,1,0:T(8,128)}, f32[1,4,16,16,64]{4,3,2,1,0:T(8,128)}, f32[4,16,16,64]{3,2,1,0:T(8,128)}...) fusion(s32[4,16,16,64]{3,2,1,0:T(8,128)S(1)} %copy-done, ...), kind=kLoop, calls=%fused_computation.79 | loop fusion | flops 3538944 | bytes 3211264 | tf_op jit(solution)/shard_map/stack | solution.py:77
  168.7 2.8 collective-permute-start.9
  174.3 8.1 %all-to-all-start.1 = ((f32[32,1,256]{2,1,0:T(1,128)}), f32[32,1,256]{2,1,0:T(1,128)}, u32[]{:S(2)}, u32[]{:S(2)}) async-start(f32[32,1,256]{2,1,0:T(1,128)} %reshape.148), calls=%async_computation.1 | async-start | bytes 65536 | tf_op jit(solution)/shard_map/all_to_all | solution.py:49
  183.5 2.3 collective-permute-done.9
  185.8 4.6 %multiply_bitcast_fusion = (f32[1,4,16,16,64]{4,3,2,1,0:T(8,128)S(1)}, f32[1,4,16,16,64]{4,3,2,1,0:T(8,128)S(1)}, f32[1,4,16,16,64]{4,3,2,1,0:T(8,128)S(1)}, f32...) fusion(f32[4,16,16,64]{3,2,1,0:T(8,128)S(1)} %copy-done.9, ...), kind=kLoop, calls=%fused_computation.158 | loop fusion | flops 5898240 | bytes 3670016 | tf_op jit(solution)/shard_map/stack | solution.py:77
  194.1 2.2 collective-permute-start.13
  196.3 5.5 %collective-permute-start.14 = (f32[3,4,2,16,64]{4,3,2,1,0:T(8,128)}, f32[3,4,2,16,64]{4,3,2,1,0:T(8,128)}, u32[]{:S(2)}, u32[]{:S(2)}) collective-permute-start(f32[3,4,2,16,64]{4,3,2,1,0:T(8,128)} %get-tuple-element.55), channel_id=1, source_target_pairs={{8,0},{16,8},{24,16},{0,24},{9,1},{17,9},{25,17},{1,25},{10,2},{18... | collective-permute-start | bytes 294920 | tf_op jit(solution)/shard_map/ppermute | solution.py:41
  203.8 2.1 reduce.1
  214.0 4.4 %multiply_reduce_fusion.2 = (f32[4]{0:T(128)S(1)}, f32[4]{0:T(128)S(1)}, f32[4]{0:T(128)S(1)}, f32[4,16,16,64]{3,2,1,0:T(8,128)}, f32[4,16,16,64]{3,2,1,0:T(8,12...) fusion(f32[4,16,16,64]{3,2,1,0:T(8,128)S(1)} %copy-done.52, ...), kind=kLoop, calls=%fused_computation.154 | loop fusion | flops 7208948 | bytes 5242928 | tf_op jit(solution)/shard_map/reduce_sum | solution.py:165
  219.1 5.1 %all-to-all-start.2 = ((f32[32,3,4]{2,1,0:T(4,128)}), f32[32,3,4]{2,1,0:T(4,128)S(1)}, u32[]{:S(2)}, u32[]{:S(2)}) async-start(f32[32,3,4]{2,1,0:T(4,128)} %broadcast_in_dim.121), calls=%async_computation.2 | async-start | bytes 131072 | tf_op jit(solution)/shard_map/all_to_all | solution.py:49
  227.1 7.7 %collective-permute-start.10 = (f32[3,2,16,16,64]{4,3,2,1,0:T(8,128)}, f32[3,2,16,16,64]{4,3,2,1,0:T(8,128)}, u32[]{:S(2)}, u32[]{:S(2)}) collective-permute-start(f32[3,2,16,16,64]{4,3,2,1,0:T(8,128)} %get-tuple-element.56), channel_id=1, source_target_pairs={{32,0},{64,32},{96,64},{128,96},{160,128},{192,160},{224,192},{256... | collective-permute-start | bytes 1179656 | tf_op jit(solution)/shard_map/ppermute | solution.py:41
  234.8 2.2 collective-permute-start.11
  237.1 11.9 %fusion = f32[4,16,16,64]{3,0,2,1:T(4,128)} fusion(s32[16,16,64]{2,1,0:T(8,128)S(1)} %copy-done.59, f32[4,64]{1,0:T(4,128)S(1)} %copy-done.62), kind=kOutput, calls=%fused_computation.1 | convolution fusion | flops 51380224 | bytes 328704 | tf_op jit(solution)/shard_map/dot_general | solution.py:123
  249.6 52.3 %collective-permute-done.10 = f32[3,2,16,16,64]{4,3,2,1,0:T(8,128)} collective-permute-done((f32[3,2,16,16,64]{4,3,2,1,0:T(8,128)}, f32[3,2,16,16,64]{4,3,2,1,0:T(8,128)}, u32[]{:S(2)}, u32[]{:S(2)}) %collective-permute-start.10) | collective-permute-done | bytes 393248 | tf_op jit(solution)/shard_map/ppermute | solution.py:41
  301.9 9.8 %collective-permute-done.11 = f32[3,2,16,16,64]{4,3,2,1,0:T(8,128)} collective-permute-done((f32[3,2,16,16,64]{4,3,2,1,0:T(8,128)}, f32[3,2,16,16,64]{4,3,2,1,0:T(8,128)}, u32[]{:S(2)}, u32[]{:S(2)}) %collective-permute-start.11) | collective-permute-done | bytes 393248 | tf_op jit(solution)/shard_map/ppermute | solution.py:40
  311.7 3.4 %fusion.35 = f32[4,16,16,64]{3,2,1,0:T(8,128)} fusion(f32[4,16,16,64]{3,2,1,0:T(8,128)S(1)} %get-tuple-element.29, f32[3,2,16,16,64]{4,3,2,1,0:T(8,128)} %collective-permute-done.11, f32[1,4,16,16,64]{4,3,2,1,0:T(8,128)S(1)} %copy-done.16, f32[1,4,16,16,64]{4,3,2,1,0:T(8,128)} %get-tuple-element.89, f32[1,4,16,16,64]{4,3,2,1,0:T(8,128)S(1)} %copy-done.2, ...), kind=kLoop, calls=%fused_computation.101 | loop fusion | flops 2818048 | bytes 3997744 | tf_op jit(solution)/shard_map/add | solution.py:162
  (211 shorter events, 53.7 us)
Async XLA Ops:
  1.8 11.4 %collective-permute-start.6 = (f32[4,16,1,64]{3,2,1,0:T(1,128)S(1)}, f32[4,16,1,64]{3,2,1,0:T(1,128)S(1)}, u32[]{:S(2)}, u32[]{:S(2)}) collective-permute-start(f32[4,16,1,64]{3,2,1,0:T(1,128)S(1)} %slice.296), channel_id=1, source_target_pairs={{0,7},{1,0},{2,1},{3,2},{4,3},{5,4},{6,5},{7,6},{8,15},{9,8},{10,9... | collective-permute-start | bytes 49160 | tf_op jit(solution)/shard_map/ppermute | solution.py:30
  2.6 10.6 %collective-permute-start.3 = (f32[4,1,16,64]{3,2,1,0:T(8,128)S(1)}, f32[4,1,16,64]{3,2,1,0:T(8,128)S(1)}, u32[]{:S(2)}, u32[]{:S(2)}) collective-permute-start(f32[4,1,16,64]{3,2,1,0:T(8,128)S(1)} %slice.285), channel_id=1, source_target_pairs={{0,24},{8,0},{16,8},{24,16},{1,25},{9,1},{17,9},{25,17},{2,26},{10... | collective-permute-start | bytes 49160 | tf_op jit(solution)/shard_map/ppermute | solution.py:30
  13.1 15.8 %copy-start.60 = (s32[16384]{0:T(1024)}, s32[16384]{0:T(1024)S(1)}, u32[]{:S(2)}) copy-start(s32[16384]{0:T(1024)S(1)} %eq.116) | copy-start | bytes 196612
  17.6 21.9 %copy-start.34 = (f32[4,16,16,64]{3,2,1,0:T(8,128)}, f32[4,16,16,64]{3,2,1,0:T(8,128)S(1)}, u32[]{:S(2)}) copy-start(f32[4,16,16,64]{3,2,1,0:T(8,128)S(1)} %get-tuple-element.101) | copy-start | bytes 786436
  19.0 20.5 %collective-permute-start = (f32[1,16,16,64]{3,2,1,0:T(8,128)S(1)}, f32[1,16,16,64]{3,2,1,0:T(8,128)}, u32[]{:S(2)}, u32[]{:S(2)}) collective-permute-start(f32[1,16,16,64]{3,2,1,0:T(8,128)S(1)} %slice.344), channel_id=1, source_target_pairs={{32,0},{64,32},{96,64},{128,96},{160,128},{192,160},{224,192},{256... | collective-permute-start | bytes 196616 | tf_op jit(solution)/shard_map/ppermute | solution.py:24
  31.8 34.9 %all-to-all-start = ((f32[32,1,256]{2,1,0:T(1,128)}), f32[32,1,256]{2,1,0:T(1,128)}, u32[]{:S(2)}, u32[]{:S(2)}) async-start(f32[32,1,256]{2,1,0:T(1,128)} %reshape.146), calls=%async_computation | async-start | bytes 65536 | tf_op jit(solution)/shard_map/all_to_all | solution.py:49
  46.1 34.8 %collective-permute-start.7 = (f32[3,4,16,2,64]{4,3,2,1,0:T(2,128)}, f32[3,4,16,2,64]{4,3,2,1,0:T(2,128)S(1)}, u32[]{:S(2)}, u32[]{:S(2)}) collective-permute-start(f32[3,4,16,2,64]{4,3,2,1,0:T(2,128)} %get-tuple-element.60), channel_id=1, source_target_pairs={{0,1},{1,2},{2,3},{3,4},{4,5},{5,6},{6,7},{7,0},{8,9},{9,10},{10,1... | collective-permute-start | bytes 294920 | tf_op jit(solution)/shard_map/ppermute | solution.py:40
  46.2 37.7 %collective-permute-start.8 = (f32[3,4,16,2,64]{4,3,2,1,0:T(2,128)}, f32[3,4,16,2,64]{4,3,2,1,0:T(2,128)}, u32[]{:S(2)}, u32[]{:S(2)}) collective-permute-start(f32[3,4,16,2,64]{4,3,2,1,0:T(2,128)} %get-tuple-element.61), channel_id=1, source_target_pairs={{1,0},{2,1},{3,2},{4,3},{5,4},{6,5},{7,6},{0,7},{9,8},{10,9},{11,1... | collective-permute-start | bytes 294920 | tf_op jit(solution)/shard_map/ppermute | solution.py:41
  48.7 37.0 %collective-permute-start.4 = (f32[3,4,2,16,64]{4,3,2,1,0:T(8,128)}, f32[3,4,2,16,64]{4,3,2,1,0:T(8,128)}, u32[]{:S(2)}, u32[]{:S(2)}) collective-permute-start(f32[3,4,2,16,64]{4,3,2,1,0:T(8,128)} %get-tuple-element.62), channel_id=1, source_target_pairs={{0,8},{8,16},{16,24},{24,0},{1,9},{9,17},{17,25},{25,1},{2,10},{10... | collective-permute-start | bytes 294920 | tf_op jit(solution)/shard_map/ppermute | solution.py:40
  52.1 33.5 %collective-permute-start.5 = (f32[3,4,2,16,64]{4,3,2,1,0:T(8,128)}, f32[3,4,2,16,64]{4,3,2,1,0:T(8,128)}, u32[]{:S(2)}, u32[]{:S(2)}) collective-permute-start(f32[3,4,2,16,64]{4,3,2,1,0:T(8,128)} %get-tuple-element.63), channel_id=1, source_target_pairs={{8,0},{16,8},{24,16},{0,24},{9,1},{17,9},{25,17},{1,25},{10,2},{18... | collective-permute-start | bytes 294920 | tf_op jit(solution)/shard_map/ppermute | solution.py:41
  59.9 75.5 %collective-permute-start.1 = (f32[3,2,16,16,64]{4,3,2,1,0:T(8,128)}, f32[3,2,16,16,64]{4,3,2,1,0:T(8,128)}, u32[]{:S(2)}, u32[]{:S(2)}) collective-permute-start(f32[3,2,16,16,64]{4,3,2,1,0:T(8,128)} %get-tuple-element.58), channel_id=1, source_target_pairs={{32,0},{64,32},{96,64},{128,96},{160,128},{192,160},{224,192},{256... | collective-permute-start | bytes 1179656 | tf_op jit(solution)/shard_map/ppermute | solution.py:41
  81.0 66.2 %collective-permute-start.2 = (f32[3,2,16,16,64]{4,3,2,1,0:T(8,128)S(1)}, f32[3,2,16,16,64]{4,3,2,1,0:T(8,128)S(1)}, u32[]{:S(2)}, u32[]{:S(2)}) collective-permute-start(f32[3,2,16,16,64]{4,3,2,1,0:T(8,128)S(1)} %copy-done.49), channel_id=1, source_target_pairs={{0,32},{32,64},{64,96},{96,128},{128,160},{160,192},{192,224},{224... | collective-permute-start | bytes 1179656 | tf_op jit(solution)/shard_map/ppermute | solution.py:40
  90.1 57.0 %copy-start.20 = (f32[1,4,16,16,64]{4,3,2,1,0:T(8,128)S(1)}, f32[1,4,16,16,64]{4,3,2,1,0:T(8,128)}, u32[]{:S(2)}) copy-start(f32[1,4,16,16,64]{4,3,2,1,0:T(8,128)} %copy-done.19) | copy-start | bytes 786436
  90.1 57.0 %copy-start.22 = (f32[1,4,16,16,64]{4,3,2,1,0:T(8,128)S(1)}, f32[1,4,16,16,64]{4,3,2,1,0:T(8,128)}, u32[]{:S(2)}) copy-start(f32[1,4,16,16,64]{4,3,2,1,0:T(8,128)} %copy-done.21) | copy-start | bytes 786436
  90.1 57.0 %copy-start.50 = (f32[16,16,64]{2,1,0:T(8,128)S(1)}, f32[16,16,64]{2,1,0:T(8,128)}, u32[]{:S(2)}) copy-start(f32[16,16,64]{2,1,0:T(8,128)} %param.17) | copy-start | bytes 196612
  90.1 57.1 %copy-start.54 = (f32[16,16,64]{2,1,0:T(8,128)S(1)}, f32[16,16,64]{2,1,0:T(8,128)}, u32[]{:S(2)}) copy-start(f32[16,16,64]{2,1,0:T(8,128)} %param.16) | copy-start | bytes 196612
  148.9 15.3 %copy-start.56 = (f32[16,16,64]{2,1,0:T(8,128)S(1)}, f32[16,16,64]{2,1,0:T(8,128)}, u32[]{:S(2)}) copy-start(f32[16,16,64]{2,1,0:T(8,128)} %param.14) | copy-start | bytes 196612
  149.0 6.8 %collective-permute-start.15 = (f32[4,16,1,64]{3,2,1,0:T(1,128)S(1)}, f32[4,16,1,64]{3,2,1,0:T(1,128)S(1)}, u32[]{:S(2)}, u32[]{:S(2)}) collective-permute-start(f32[4,16,1,64]{3,2,1,0:T(1,128)S(1)} %slice.386), channel_id=1, source_target_pairs={{0,7},{1,0},{2,1},{3,2},{4,3},{5,4},{6,5},{7,6},{8,15},{9,8},{10,9... | collective-permute-start | bytes 49160 | tf_op jit(solution)/shard_map/ppermute | solution.py:30
  149.4 14.8 %collective-permute-start.12 = (f32[4,1,16,64]{3,2,1,0:T(8,128)S(1)}, f32[4,1,16,64]{3,2,1,0:T(8,128)S(1)}, u32[]{:S(2)}, u32[]{:S(2)}) collective-permute-start(f32[4,1,16,64]{3,2,1,0:T(8,128)S(1)} %slice.378), channel_id=1, source_target_pairs={{0,24},{8,0},{16,8},{24,16},{1,25},{9,1},{17,9},{25,17},{2,26},{10... | collective-permute-start | bytes 49160 | tf_op jit(solution)/shard_map/ppermute | solution.py:30
  168.7 17.1 %copy-start.15 = (f32[4,16,16,64]{3,2,1,0:T(8,128)}, f32[4,16,16,64]{3,2,1,0:T(8,128)S(1)}, u32[]{:S(2)}) copy-start(f32[4,16,16,64]{3,2,1,0:T(8,128)S(1)} %get-tuple-element.96) | copy-start | bytes 786436
  168.7 17.1 %copy-start.17 = (f32[4,16,16,64]{3,2,1,0:T(8,128)}, f32[4,16,16,64]{3,2,1,0:T(8,128)S(1)}, u32[]{:S(2)}) copy-start(f32[4,16,16,64]{3,2,1,0:T(8,128)S(1)} %get-tuple-element.68) | copy-start | bytes 786436
  168.7 17.1 %collective-permute-start.9 = (f32[1,16,16,64]{3,2,1,0:T(8,128)S(1)}, f32[1,16,16,64]{3,2,1,0:T(8,128)S(1)}, u32[]{:S(2)}, u32[]{:S(2)}) collective-permute-start(f32[1,16,16,64]{3,2,1,0:T(8,128)S(1)} %slice.366), channel_id=1, source_target_pairs={{32,0},{64,32},{96,64},{128,96},{160,128},{192,160},{224,192},{256... | collective-permute-start | bytes 196616 | tf_op jit(solution)/shard_map/ppermute | solution.py:24
  174.3 29.5 %all-to-all-start.1 = ((f32[32,1,256]{2,1,0:T(1,128)}), f32[32,1,256]{2,1,0:T(1,128)}, u32[]{:S(2)}, u32[]{:S(2)}) async-start(f32[32,1,256]{2,1,0:T(1,128)} %reshape.148), calls=%async_computation.1 | async-start | bytes 65536 | tf_op jit(solution)/shard_map/all_to_all | solution.py:49
  191.5 15.8 %collective-permute-start.16 = (f32[3,4,16,2,64]{4,3,2,1,0:T(2,128)}, f32[3,4,16,2,64]{4,3,2,1,0:T(2,128)S(1)}, u32[]{:S(2)}, u32[]{:S(2)}) collective-permute-start(f32[3,4,16,2,64]{4,3,2,1,0:T(2,128)} %get-tuple-element.52), channel_id=1, source_target_pairs={{0,1},{1,2},{2,3},{3,4},{4,5},{5,6},{6,7},{7,0},{8,9},{9,10},{10,1... | collective-permute-start | bytes 294920 | tf_op jit(solution)/shard_map/ppermute | solution.py:40
  191.5 15.8 %collective-permute-start.17 = (f32[3,4,16,2,64]{4,3,2,1,0:T(2,128)}, f32[3,4,16,2,64]{4,3,2,1,0:T(2,128)}, u32[]{:S(2)}, u32[]{:S(2)}) collective-permute-start(f32[3,4,16,2,64]{4,3,2,1,0:T(2,128)} %get-tuple-element.53), channel_id=1, source_target_pairs={{1,0},{2,1},{3,2},{4,3},{5,4},{6,5},{7,6},{0,7},{9,8},{10,9},{11,1... | collective-permute-start | bytes 294920 | tf_op jit(solution)/shard_map/ppermute | solution.py:41
  194.1 15.4 %collective-permute-start.13 = (f32[3,4,2,16,64]{4,3,2,1,0:T(8,128)}, f32[3,4,2,16,64]{4,3,2,1,0:T(8,128)}, u32[]{:S(2)}, u32[]{:S(2)}) collective-permute-start(f32[3,4,2,16,64]{4,3,2,1,0:T(8,128)} %get-tuple-element.54), channel_id=1, source_target_pairs={{0,8},{8,16},{16,24},{24,0},{1,9},{9,17},{17,25},{25,1},{2,10},{10... | collective-permute-start | bytes 294920 | tf_op jit(solution)/shard_map/ppermute | solution.py:40
  196.3 13.2 %collective-permute-start.14 = (f32[3,4,2,16,64]{4,3,2,1,0:T(8,128)}, f32[3,4,2,16,64]{4,3,2,1,0:T(8,128)}, u32[]{:S(2)}, u32[]{:S(2)}) collective-permute-start(f32[3,4,2,16,64]{4,3,2,1,0:T(8,128)} %get-tuple-element.55), channel_id=1, source_target_pairs={{8,0},{16,8},{24,16},{0,24},{9,1},{17,9},{25,17},{1,25},{10,2},{18... | collective-permute-start | bytes 294920 | tf_op jit(solution)/shard_map/ppermute | solution.py:41
  219.1 29.8 %all-to-all-start.2 = ((f32[32,3,4]{2,1,0:T(4,128)}), f32[32,3,4]{2,1,0:T(4,128)S(1)}, u32[]{:S(2)}, u32[]{:S(2)}) async-start(f32[32,3,4]{2,1,0:T(4,128)} %broadcast_in_dim.121), calls=%async_computation.2 | async-start | bytes 131072 | tf_op jit(solution)/shard_map/all_to_all | solution.py:49
  227.1 84.6 %copy-start.2 = (f32[1,4,16,16,64]{4,3,2,1,0:T(8,128)S(1)}, f32[1,4,16,16,64]{4,3,2,1,0:T(8,128)}, u32[]{:S(2)}) copy-start(f32[1,4,16,16,64]{4,3,2,1,0:T(8,128)} %get-tuple-element.94) | copy-start | bytes 786436
  227.1 84.6 %copy-start.16 = (f32[1,4,16,16,64]{4,3,2,1,0:T(8,128)S(1)}, f32[1,4,16,16,64]{4,3,2,1,0:T(8,128)}, u32[]{:S(2)}) copy-start(f32[1,4,16,16,64]{4,3,2,1,0:T(8,128)} %get-tuple-element.88) | copy-start | bytes 786436
  227.1 74.7 %collective-permute-start.10 = (f32[3,2,16,16,64]{4,3,2,1,0:T(8,128)}, f32[3,2,16,16,64]{4,3,2,1,0:T(8,128)}, u32[]{:S(2)}, u32[]{:S(2)}) collective-permute-start(f32[3,2,16,16,64]{4,3,2,1,0:T(8,128)} %get-tuple-element.56), channel_id=1, source_target_pairs={{32,0},{64,32},{96,64},{128,96},{160,128},{192,160},{224,192},{256... | collective-permute-start | bytes 1179656 | tf_op jit(solution)/shard_map/ppermute | solution.py:41
  234.8 76.9 %collective-permute-start.11 = (f32[3,2,16,16,64]{4,3,2,1,0:T(8,128)}, f32[3,2,16,16,64]{4,3,2,1,0:T(8,128)}, u32[]{:S(2)}, u32[]{:S(2)}) collective-permute-start(f32[3,2,16,16,64]{4,3,2,1,0:T(8,128)} %get-tuple-element.57), channel_id=1, source_target_pairs={{0,32},{32,64},{64,96},{96,128},{128,160},{160,192},{192,224},{224... | collective-permute-start | bytes 1179656 | tf_op jit(solution)/shard_map/ppermute | solution.py:40
  (54 other events, 272.8 us)

commit v2 on v0

v2 whole, which is shorter than its diff:
```python
import functools

import jax
import jax.numpy as jnp
from jax import lax
from jax.experimental import pallas as pl
from jax.experimental.pallas import tpu as pltpu
from jax.sharding import PartitionSpec as P


KX = 64
KY = 64
KZ = 128
SHELLS = 64
X = 4
R = 8
Z = 16
L = 128
HALF = 64
time_step = 0.25
F32 = jnp.float32
BF16 = jnp.bfloat16
FULL = (X, R, Z, L)
VMEM_LIMIT = 24 * 1024 * 1024


def lanes(shape):
    return lax.broadcasted_iota(jnp.int32, shape, len(shape) - 1)


def pack(low, high):
    return jnp.concatenate([low, high], axis=-1)


def swap(row):
    return pltpu.roll(row, HALF, row.ndim - 1)


def split6(code):
    whole = jnp.floor((code + 0.5) * (1.0 / 6.0))
    return whole, code - 6.0 * whole


def digits_of(code):
    rest, pos = split6(code)
    rest, ky = split6(rest)
    kx, kz = split6(rest)
    return pos, ky, kz, kx


def c_low(digit):
    return jnp.where(digit == 1.0, -0.5, 0.0)


def c_far(digit):
    return jnp.where(digit == 4.0, -0.5, 0.0)


def c_high(digit):
    return jnp.where(digit == 5.0, 0.5, jnp.maximum(0.5 * digit - 0.5, 0.0))


def terms(digit, differ):
    half = -0.5 * differ
    low = jnp.where(digit == 1.0, half, 0.0)
    far = jnp.where(digit == 4.0, half, 0.0)
    high = c_high(digit) * differ
    return low, differ - low - high - far, high, far


def coeffs(digit):
    low, high, far = c_low(digit), c_high(digit), c_far(digit)
    return low, 1.0 - low - high - far, high, far


class Shifts:
    def __init__(self):
        lane = lanes((Z, L))
        self.low = lane < HALF
        kx = lane & (HALF - 1)
        self.kx_first, self.kx_second = kx == 0, kx < 2
        self.kx_last, self.kx_pair = kx == HALF - 1, kx >= HALF - 2
        z = lax.broadcasted_iota(jnp.int32, (Z, L), 0)
        self.z0, self.z1 = z == 0, z == 1
        self.z_last, self.z_before = z == Z - 1, z == Z - 2

    def kx(self, row, by):
        mask, wrapped = {
            -1: (self.kx_last, HALF - 1),
            -2: (self.kx_pair, HALF - 2),
            1: (self.kx_first, HALF + 1),
            2: (self.kx_second, HALF + 2),
        }[by]
        return jnp.where(mask, pltpu.roll(row, wrapped, 1), pltpu.roll(row, by % L, 1))

    def kz_next(self, row, after):
        return jnp.where(self.z_last, after, pltpu.roll(row, Z - 1, 0))

    def kz_next2(self, row, after, after2):
        return jnp.where(self.z_last, after2, jnp.where(self.z_before, after, pltpu.roll(row, Z - 2, 0)))

    def kz_prev(self, row, before):
        return jnp.where(self.z0, before, pltpu.roll(row, 1, 0))

    def kz_prev2(self, row, before, before2):
        return jnp.where(self.z0, before2, jnp.where(self.z1, before, pltpu.roll(row, 2, 0)))


def ky_up_rows(array):
    return array, swap(array)


def ky_down_rows(array):
    return swap(array), array


def along_kx(sh, u, digit):
    low, centre, high, far = terms(digit, u - sh.kx(u, -1))
    return sh.kx(low, -1) + centre + sh.kx(high, 1) + sh.kx(far, 2)


def along_kz(sh, u, digit, above, t_above, digit_b, below, s_below):
    low, centre, high, far = terms(digit, u - sh.kz_next(u, above))
    edge = below - u[0:1]
    return (
        sh.kz_next(low, t_above)
        + centre
        + sh.kz_prev(high, c_high(digit_b) * edge)
        + sh.kz_prev2(far, c_far(digit_b) * edge, s_below)
    )


def along_ky(sh, rows, digit_rows, above, t_above, digit_b, below, s_below):
    nxt = rows[1:] + [jnp.where(sh.low, swap(rows[0]), above)]
    parts = [terms(digit_rows[r], rows[r] - nxt[r]) for r in range(R)]
    edge = below - rows[0]
    low_after = jnp.where(sh.low, swap(parts[0][0]), t_above)
    high_before = jnp.where(sh.low, c_high(digit_b) * edge, swap(parts[R - 1][2]))
    far_before = jnp.where(sh.low, c_far(digit_b) * edge, swap(parts[R - 1][3]))
    far_before2 = jnp.where(sh.low, s_below, swap(parts[R - 2][3]))
    lows = [p[0] for p in parts] + [low_after]
    highs = [high_before] + [p[2] for p in parts]
    fars = [far_before2, far_before] + [p[3] for p in parts]
    return [lows[r + 1] + parts[r][1] + highs[r] + fars[r] for r in range(R)]


def gather(table, index):
    wide = jnp.broadcast_to(table, (Z, L))
    return jnp.take_along_axis(wide, index, axis=1)


def pos_terms(rows, digit_rows):
    nxt = rows[1:] + [None]
    parts = [
        terms(digit_rows[x], rows[x] - nxt[x] if nxt[x] is not None else rows[x])
        for x in range(X)
    ]
    out = []
    for x in range(X):
        value = parts[x][1]
        if x + 1 < X:
            value = value + parts[x + 1][0]
        if x >= 1:
            value = value + parts[x - 1][2]
        if x >= 2:
            value = value + parts[x - 2][3]
        out.append(value)
    return out


def pos_corrections(first, digit_last, digit_b, below, s_below, above, t_above):
    edge = below - first
    low, centre, _, _ = coeffs(digit_last)
    return (
        c_high(digit_b) * edge + s_below,
        c_far(digit_b) * edge,
        -low * above,
        t_above - centre * above,
    )


def shell_sums(w_ref, shell_ref):
    shells = lax.broadcasted_iota(jnp.int32, (SHELLS, L), 0)

    def body(r, total):
        left = jnp.concatenate(
            [w_ref[r, pl.ds(z, 2 * X, stride=Z), :] for z in range(Z)], axis=1
        ).astype(BF16)
        right = jnp.concatenate(
            [
                jnp.where(shells == shell_ref[r, z : z + 1, :], 1.0, 0.0).astype(BF16)
                for z in range(Z)
            ],
            axis=1,
        )
        return total + lax.dot_general(
            left, right, (((1,), (1,)), ((), ())), preferred_element_type=F32
        )

    both = lax.fori_loop(0, R, body, jnp.zeros((2 * X, SHELLS), F32))
    return both[:X] + both[X:]


def put_weighted(w_ref, r, x, value):
    head = value.astype(BF16).astype(F32)
    w_ref[r, x * Z : (x + 1) * Z, :] = head
    w_ref[r, (X + x) * Z : (X + x + 1) * Z, :] = value - head


def edges_kernel(u_ref, code_ref, start_ref, vel_ref, pos_up, pos_down, ky_up, ky_down, kz_up, kz_down):
    def whole(ref, x, r):
        return pack(ref[x, r], ref[x, r + R])

    def plane(ref, x, z):
        both = ref[x, :, z, :]
        return pack(both[:R], both[R:])

    for r in range(R):
        v = pack(vel_ref[r], vel_ref[r + R])
        u0, u1, u2, u3 = (v * whole(u_ref, x, r) for x in range(X))
        d0, d2, d3 = (split6(whole(code_ref, x, r).astype(F32))[1] for x in (0, 2, 3))
        pos_up[0, r] = d3
        pos_up[1, r] = u3
        pos_up[2, r] = c_far(d2) * (u2 - u3)
        pos_down[0, r] = u0
        pos_down[1, r] = c_low(d0) * (u0 - u1)
    for x in range(X):
        k = 2 * R - 1
        d_last = digits_of(code_ref[x, k].astype(F32))[1]
        d_prev = digits_of(code_ref[x, k - 1].astype(F32))[1]
        last, prev = u_ref[x, k], u_ref[x, k - 1]
        ky_up[0, x] = pack(d_last, last)
        ky_up[1, x] = pack(c_far(d_prev) * (prev - last), start_ref[x, k])
        ky_up[2, x] = pack(start_ref[x, k - 1], start_ref[x, k - 1])
        d_first = digits_of(code_ref[x, 0].astype(F32))[1]
        first, second = u_ref[x, 0], u_ref[x, 1]
        ky_down[0, x] = pack(first, c_low(d_first) * (first - second))
        ky_down[1, x] = pack(start_ref[x, 0], start_ref[x, 1])
        d_last = digits_of(plane(code_ref, x, Z - 1).astype(F32))[2]
        d_prev = digits_of(plane(code_ref, x, Z - 2).astype(F32))[2]
        last, prev = plane(u_ref, x, Z - 1), plane(u_ref, x, Z - 2)
        kz_up[0, x] = d_last
        kz_up[1, x] = last
        kz_up[2, x] = c_far(d_prev) * (prev - last)
        kz_up[3, x] = plane(start_ref, x, Z - 1)
        kz_up[4, x] = plane(start_ref, x, Z - 2)
        d_first = digits_of(plane(code_ref, x, 0).astype(F32))[2]
        first, second = plane(u_ref, x, 0), plane(u_ref, x, 1)
        kz_down[0, x] = first
        kz_down[1, x] = c_low(d_first) * (first - second)
        kz_down[2, x] = plane(start_ref, x, 0)
        kz_down[3, x] = plane(start_ref, x, 1)


def first_sums_kernel(u_ref, code_ref, vel_ref, shell_ref, out_ref, in_ref, u_p, code_p, fields_p, shell_p, sums, w_ref):
    for r in range(R):
        fields_p[0, r] = pack(vel_ref[r], vel_ref[r + R])
        weight = pack(out_ref[r], out_ref[r + R])
        fields_p[1, r] = weight
        fields_p[2, r] = pack(in_ref[r], in_ref[r + R])
        shell_p[r] = pack(shell_ref[r], shell_ref[r + R])
        for x in range(X):
            u = pack(u_ref[x, r], u_ref[x, r + R])
            u_p[x, r] = u
            code_p[x, r] = pack(code_ref[x, r], code_ref[x, r + R]).astype(F32)
            put_weighted(w_ref, r, x, weight * u)
    totals = shell_sums(w_ref, shell_p)
    tile = jnp.concatenate([totals, jnp.zeros_like(totals)], axis=1)
    for n in range(sums.shape[0]):
        sums[n] = tile


def add_copies(got):
    total = got[0]
    for n in range(1, got.shape[0]):
        total = total + got[n]
    return total


def momentum_terms(sh, field, x, u, digit, k_ky, kz_rows):
    ks = (along_kx(sh, u, digit[3]), k_ky, along_kz(sh, u, digit[2], *kz_rows))
    return ks, field[0, x] * ks[0] + field[1, x] * ks[1] + field[2, x] * ks[2]


def face(digit, f_prev, f, f_next, f_next2):
    low, centre, high, far = coeffs(digit)
    return low * f_prev + centre * f + high * f_next + far * f_next2


def section_kernel(
    field, u_p, code_p, fields_p, shell_p, section_ref, start_ref, got_sums,
    ky_up, ky_down, kz_up, kz_down,
    partial, slopes, grads,
):
    sh = Shifts()
    totals = add_copies(got_sums)

    def body(x, carry):
        rows = [u_p[x, r] for r in range(R)]
        digit = [digits_of(code_p[x, r]) for r in range(R)]
        start = [pack(start_ref[x, r], start_ref[x, r + R]) for r in range(R)]
        d_b, below = ky_up_rows(ky_up[0, x])
        s_below, f_below = ky_up_rows(ky_up[1, x])
        f_below2 = ky_up[2, x]
        above, t_above = ky_down_rows(ky_down[0, x])
        f_above, f_above2 = ky_down_rows(ky_down[1, x])
        k_ky = along_ky(sh, rows, [d[1] for d in digit], above, t_above, d_b, below, s_below)
        before = [jnp.where(sh.low, f_below, swap(start[R - 1]))] + start[:-1]
        after = start + [
            jnp.where(sh.low, swap(start[0]), f_above),
            jnp.where(sh.low, swap(start[1]), f_above2),
        ]
        faces = [face(digit[r][1], before[r], start[r], after[r + 1], after[r + 2]) for r in range(R)]
        face_b = face(d_b, f_below2, f_below, start[0], start[1])
        faces_before = [jnp.where(sh.low, face_b, swap(faces[R - 1]))] + faces[:-1]
        grad_x = [jnp.zeros((Z, L), F32)] * 3
        for r in range(R):
            u, f, d = rows[r], start[r], digit[r]
            up = [kz_up[n, x, r : r + 1, :] for n in range(5)]
            down = [kz_down[n, x, r : r + 1, :] for n in range(4)]
            ks, push = momentum_terms(sh, field, x, u, d, k_ky[r], (down[0], down[1], up[0], up[1], up[2]))
            sec = pack(section_ref[x, r], section_ref[x, r + R])
            grad_x = [g + sec * k for g, k in zip(grad_x, ks)]
            partial[x, r] = push
            faces_kx = face(d[3], sh.kx(f, 1), f, sh.kx(f, -1), sh.kx(f, -2))
            slopes[0, x, r] = faces_kx - sh.kx(faces_kx, 1)
            slopes[1, x, r] = faces[r] - faces_before[r]
            faces_kz = face(
                d[2], sh.kz_prev(f, up[3]), f, sh.kz_next(f, down[2]), sh.kz_next2(f, down[2], down[3])
            )
            slopes[2, x, r] = faces_kz - sh.kz_prev(faces_kz, face(up[0], up[4], up[3], f[0:1], f[1:2]))
        for c in range(3):
            grads[c, x] = grad_x[c]
        return carry

    lax.fori_loop(0, X, body, 0)

    def finish(r, carry):
        v, back, shell = fields_p[0, r], fields_p[2, r], shell_p[r]
        us = [u_p[x, r] for x in range(X)]
        k_pos = pos_terms([v * u for u in us], [split6(code_p[x, r])[1] for x in range(X)])
        for x in range(X):
            applied = back * gather(totals[x : x + 1], shell) - partial[x, r] - k_pos[x] - us[x]
            partial[x, r] = 0.5 * us[x] + (0.5 * time_step) * applied
        return carry

    lax.fori_loop(0, R, finish, 0)


def section_edges_kernel(partial, u_p, code_p, fields_p, got_up, got_down, section, pos_up, pos_down):
    def body(r, carry):
        v = fields_p[0, r]
        d0, d2, d3 = (split6(code_p[x, r])[1] for x in (0, 2, 3))
        more = pos_corrections(
            v * u_p[0, r], d3, got_up[0, r], got_up[1, r], got_up[2, r], got_down[0, r], got_down[1, r]
        )
        m = []
        for x in range(X):
            value = partial[x, r] - (0.5 * time_step) * more[x]
            section[x, r] = value
            m.append(v * value)
        pos_up[0, r] = m[3]
        pos_up[1, r] = c_far(d2) * (m[2] - m[3])
        pos_down[0, r] = m[0]
        pos_down[1, r] = c_low(d0) * (m[0] - m[1])
        return carry

    lax.fori_loop(0, R, body, 0)


def momentum_edges_kernel(section, code_p, ky_up, ky_down, kz_up, kz_down):
    low_half = lanes((Z, L)) < HALF
    for x in range(X):
        last, prev = section[x, R - 1], section[x, R - 2]
        far = c_far(digits_of(code_p[x, R - 2])[1]) * (prev - last)
        ky_up[x] = jnp.where(low_half, swap(last), far)
        first, second = section[x, 0], section[x, 1]
        low = c_low(digits_of(code_p[x, 0])[1]) * (first - second)
        ky_down[x] = jnp.where(low_half, first, swap(low))
        last, prev = section[x, :, Z - 1, :], section[x, :, Z - 2, :]
        kz_up[0, x] = last
        kz_up[1, x] = c_far(digits_of(code_p[x, :, Z - 2, :])[2]) * (prev - last)
        first, second = section[x, :, 0, :], section[x, :, 1, :]
        kz_down[0, x] = first
        kz_down[1, x] = c_low(digits_of(code_p[x, :, 0, :])[2]) * (first - second)


def second_sums_kernel(section, fields_p, shell_p, slopes, grads, sums, w_ref):
    row = lax.broadcasted_iota(jnp.int32, (X, SHELLS), 0)
    column = lax.broadcasted_iota(jnp.int32, (X, SHELLS), 1)
    inner = jnp.zeros((X, SHELLS), F32)
    for x in range(X):
        parts = [(0.5 * time_step) * grads[c, x] for c in range(3)]
        for r in range(R):
            value = section[x, r]
            put_weighted(w_ref, r, x, fields_p[1, r] * value)
            parts = [p + time_step * (value * slopes[c, x, r]) for c, p in enumerate(parts)]
        for c in range(3):
            whole = jnp.sum(jnp.sum(parts[c], axis=0, keepdims=True), axis=1, keepdims=True)
            inner = inner - jnp.where((row == x) & (column == c), whole, 0.0)
    tile = jnp.concatenate([shell_sums(w_ref, shell_p), inner], axis=1)
    for n in range(sums.shape[0]):
        sums[n] = tile


def interior_kernel(field, section, u_p, code_p, fields_p, first_up, first_kz, ky_up, ky_down, kz_up, kz_down, partial):
    sh = Shifts()

    def body(x, carry):
        rows = [section[x, r] for r in range(R)]
        digit = [digits_of(code_p[x, r]) for r in range(R)]
        below, s_below = ky_up_rows(ky_up[x])
        above, t_above = ky_down_rows(ky_down[x])
        k_ky = along_ky(sh, rows, [d[1] for d in digit], above, t_above, first_up[0, x], below, s_below)
        for r in range(R):
            here = slice(r, r + 1)
            kz_rows = (
                kz_down[0, x, here, :],
                kz_down[1, x, here, :],
                first_kz[0, x, here, :],
                kz_up[0, x, here, :],
                kz_up[1, x, here, :],
            )
            _, push = momentum_terms(sh, field, x, rows[r], digit[r], k_ky[r], kz_rows)
            partial[x, r] = push
        return carry

    lax.fori_loop(0, X, body, 0)

    def finish(r, carry):
        v = fields_p[0, r]
        ms = [section[x, r] for x in range(X)]
        k_pos = pos_terms([v * m for m in ms], [split6(code_p[x, r])[1] for x in range(X)])
        for x in range(X):
            partial[x, r] = (
                0.5 * u_p[x, r] + ms[x] - time_step * (partial[x, r] + k_pos[x] + ms[x])
            )
        return carry

    lax.fori_loop(0, R, finish, 0)


def result_kernel(
    scale, partial, section, code_p, fields_p, shell_p, first_up, got_up, got_down, got_sums, state, grad
):
    totals = add_copies(got_sums)
    for r in range(R):
        v, back, shell = fields_p[0, r], fields_p[2, r], shell_p[r]
        more = pos_corrections(
            v * section[0, r], split6(code_p[3, r])[1], first_up[0, r], got_up[0, r], got_up[1, r],
            got_down[0, r], got_down[1, r],
        )
        for x in range(X):
            value = partial[x, r] + time_step * (back * gather(totals[x : x + 1], shell) - more[x])
            state[x, r] = value[:, :HALF]
            state[x, r + R] = value[:, HALF:]
    row = lax.broadcasted_iota(jnp.int32, (X, L), 0)
    column = lanes((X, L))
    for c in range(3):
        spread = jnp.broadcast_to(totals[:, SHELLS + c : SHELLS + c + 1], (X, L))
        line = jnp.sum(jnp.where(row == column, spread, 0.0), axis=0, keepdims=True)
        grad[c : c + 1, :] = line[:, :X] * scale


def call(kernel, outs, args, scalars=0, scratch=(), ops=0):
    shapes = [jax.ShapeDtypeStruct(shape, F32 if dtype is None else dtype) for shape, dtype in outs]
    moved = sum(4 * a.size for a in args) + sum(4 * s.size for s in shapes)
    vmem = pl.BlockSpec(memory_space=pltpu.VMEM)
    smem = pl.BlockSpec(memory_space=pltpu.SMEM)
    return pl.pallas_call(
        kernel,
        out_shape=shapes,
        in_specs=[smem] * scalars + [vmem] * (len(args) - scalars),
        out_specs=[vmem] * len(shapes),
        scratch_shapes=list(scratch),
        compiler_params=pltpu.CompilerParams(vmem_limit_bytes=VMEM_LIMIT),
        cost_estimate=pl.CostEstimate(flops=ops, bytes_accessed=moved, transcendentals=0),
    )(*args)


def shift(array, axis, by, wrap=True):
    count = lax.axis_size(axis)
    pairs = [(i, (i + by) % count) for i in range(count) if wrap or 0 <= i + by < count]
    return lax.ppermute(array, axis, pairs)


def shift_both(up, down, axis, wrap=True):
    up = shift(up, axis, 1, wrap)
    down = shift(down, axis, -1, wrap)
    return up, down


def exchange(copies):
    return lax.all_to_all(copies, ("ky", "kz"), 0, 0)


def shards(
    cotangent,
    start_state,
    section_state,
    face_codes,
    field_strength,
    velocity,
    shell_index,
    shell_out,
    shell_in,
):
    members = lax.axis_size("ky") * lax.axis_size("kz")
    plane, ky_plane, kz_plane = (R, Z, L), (X, Z, L), (X, R, L)
    w_scratch = [pltpu.VMEM((R, 2 * X * Z, L), F32)]
    sums_shape = ((members, X, L), None)
    up, down, ky_up, ky_down, kz_up, kz_down = call(
        edges_kernel,
        [((3,) + plane, None), ((2,) + plane, None), ((3,) + ky_plane, None), ((2,) + ky_plane, None),
         ((5,) + kz_plane, None), ((4,) + kz_plane, None)],
        [cotangent, face_codes, start_state, velocity],
        ops=4_000_000,
    )
    cotangent, up, down, ky_up, ky_down, kz_up, kz_down = lax.optimization_barrier(
        (cotangent, up, down, ky_up, ky_down, kz_up, kz_down)
    )
    up, down = shift_both(up, down, "pos", False)
    ky_up, ky_down = shift_both(ky_up, ky_down, "ky")
    kz_up, kz_down = shift_both(kz_up, kz_down, "kz")
    u_p, code_p, fields_p, shell_p, sums = call(
        first_sums_kernel,
        [(FULL, None), (FULL, None), ((3,) + plane, None), (plane, jnp.int32), sums_shape],
        [cotangent, face_codes, velocity, shell_index, shell_out, shell_in],
        scratch=w_scratch,
        ops=8_000_000,
    )
    sums = exchange(sums)
    partial, slopes, grads = call(
        section_kernel,
        [(FULL, None), ((3,) + FULL, None), ((3, X, Z, L), None)],
        [field_strength, u_p, code_p, fields_p, shell_p, section_state, start_state, sums, ky_up, ky_down, kz_up, kz_down],
        scalars=1,
        ops=16_000_000,
    )
    section, up2, down2 = call(
        section_edges_kernel,
        [(FULL, None), ((2,) + plane, None), ((2,) + plane, None)],
        [partial, u_p, code_p, fields_p, up, down],
        ops=2_000_000,
    )
    up2, down2 = shift_both(up2, down2, "pos", False)
    ky_up2, ky_down2, kz_up2, kz_down2 = call(
        momentum_edges_kernel,
        [(ky_plane, None), (ky_plane, None), ((2,) + kz_plane, None), ((2,) + kz_plane, None)],
        [section, code_p],
        ops=1_000_000,
    )
    section, ky_up2, ky_down2, kz_up2, kz_down2 = lax.optimization_barrier(
        (section, ky_up2, ky_down2, kz_up2, kz_down2)
    )
    ky_up2, ky_down2 = shift_both(ky_up2, ky_down2, "ky")
    kz_up2, kz_down2 = shift_both(kz_up2, kz_down2, "kz")
    (sums2,) = call(
        second_sums_kernel, [sums_shape], [section, fields_p, shell_p, slopes, grads], scratch=w_scratch, ops=4_000_000
    )
    sums2 = exchange(sums2)
    (partial2,) = call(
        interior_kernel,
        [(FULL, None)],
        [field_strength, section, u_p, code_p, fields_p, ky_up, kz_up, ky_up2, ky_down2, kz_up2, kz_down2],
        scalars=1,
        ops=8_000_000,
    )
    state_adjoint, field_grad = call(
        functools.partial(result_kernel, 1.0 / (KX * KY * KZ) ** 0.5),
        [((X, 2 * R, Z, HALF), None), ((3, X), None)],
        [partial2, section, code_p, fields_p, shell_p, up, up2, down2, sums2],
        ops=3_000_000,
    )
    return (state_adjoint, field_grad)


def solution(mesh):
    return jax.shard_map(
        shards,
        mesh=mesh,
        in_specs=(
            P("pos", "ky", "kz", None),
            P("pos", "ky", "kz", None),
            P("pos", "ky", "kz", None),
            P("pos", "ky", "kz", None),
            P(None, "pos"),
            P("ky", "kz", None),
            P("ky", "kz", None),
            P("ky", "kz", None),
            P("ky", "kz", None),
        ),
        out_specs=(P("pos", "ky", "kz", None), P(None, "pos")),
        check_vma=False,
    )
```

time: 402 us -> 101 us (0.25)
  the two profiles are of different devices: /device:TPU:8 before, /device:TPU:15 now
where the time goes in v2:
time: 101 us; the launch traced here: 100 us
  starting transfers between devices  57 us (56%)
  waiting for transfers between devices  22.3 us (22%)
  Pallas kernels  14.7 us (15%)
  local copies, waits for them, and re-layouts  5.32 us (5%)
    ppermute x12, starting transfers between devices, shift(): return lax.ppermute(array, axis, pairs)  39.4 us
    ppermute x12, waiting for transfers between devices, shift(): return lax.ppermute(array, axis, pairs)  22.3 us
    all_to_all x2, starting transfers between devices, exchange(): return lax.all_to_all(copies, ('ky', 'kz'), 0, 0)  17.5 us
    pallas_call x8, Pallas kernels, call(): pl.pallas_call(kernel, out_shape=shapes, in_specs=[smem] * scalars + [vme...  14.7 us
    unnamed x20, local copies, waits for them, and re-layouts  5.32 us
  transfers between devices with their start and end apart: 14, of which 4 were waited for; matrix products, arithmetic and copies ran while one was open for 0% of the time, Pallas kernels for 8%

profile of v2, /device:TPU:15, one launch (start us, length us, event | category | flops | bytes accessed | tf_op | source)
XLA Modules:
  0.0 100.1 jit_solution(9628729875533617850)
XLA Ops:
  0.6 1.0 %copy-done = f32[4,16,16,64]{3,2,1,0:T(8,128)S(1)} copy-done((f32[4,16,16,64]{3,2,1,0:T(8,128)S(1)}, f32[4,16,16,64]{3,2,1,0:T(8,128)}, u32[]{:S(2)}) %copy-start) | copy-done | bytes 262168
  1.7 1.0 %copy-done.1 = s32[4,16,16,64]{3,2,1,0:T(8,128)S(1)} copy-done((s32[4,16,16,64]{3,2,1,0:T(8,128)S(1)}, s32[4,16,16,64]{3,2,1,0:T(8,128)}, u32[]{:S(2)}) %copy-start.1) | copy-done | bytes 262168
  2.7 1.0 %copy-done.2 = f32[4,16,16,64]{3,2,1,0:T(8,128)S(1)} copy-done((f32[4,16,16,64]{3,2,1,0:T(8,128)S(1)}, f32[4,16,16,64]{3,2,1,0:T(8,128)}, u32[]{:S(2)}) %copy-start.2) | copy-done | bytes 262168
  3.8 0.9 copy-done.5
  4.7 0.4 shard_map.104
  5.1 0.5 copy-done.6
  5.7 2.4 %shard_map.105 = (f32[4,8,16,128]{3,2,1,0:T(8,128)S(1)}, f32[4,8,16,128]{3,2,1,0:T(8,128)S(1)}, f32[3,8,16,128]{3,2,1,0:T(8,128)S(1)}, s32[8,16,128]{2,1,0:T(8,128)S(1)}, f32[32,4,128]{2,1,0:T(4,128)}) custom-call(f32[4,16,16,64]{3,2,1,0:T(8,128)S(1)} %copy-done, s32[4,16,16,64]{3,2,1,0:T(8,128)S(1)} %copy-done.1, f32[16,16,64]{2,1,0:T(8,128)S(1)} %copy-done.5, ...), custom_call_target="tpu_custom_call" | custom-call | flops 8000000 | bytes 1638400 | tf_op jit(solution)/shard_map/pallas_call | solution.py:470
  8.1 9.3 %all-to-all-start = ((f32[32,4,128]{2,1,0:T(4,128)}), f32[32,4,128]{2,1,0:T(4,128)S(1)}, u32[]{:S(2)}, u32[]{:S(2)}) async-start(f32[32,4,128]{2,1,0:T(4,128)} %get-tuple-element.46), calls=%async_computation | async-start | bytes 131072 | tf_op jit(solution)/shard_map/all_to_all | solution.py:494
  17.4 8.8 %collective-permute-start.4 = (f32[3,8,16,128]{3,2,1,0:T(8,128)S(1)}, f32[3,8,16,128]{3,2,1,0:T(8,128)S(1)}, u32[]{:S(2)}, u32[]{:S(2)}) collective-permute-start(f32[3,8,16,128]{3,2,1,0:T(8,128)S(1)} %get-tuple-element.52), channel_id=1, source_target_pairs={{0,32},{32,64},{64,96},{96,128},{128,160},{160,192},{192,224},{224... | collective-permute-start | bytes 589832 | tf_op jit(solution)/shard_map/ppermute | solution.py:484
  26.2 5.0 %collective-permute-start.1 = (f32[2,4,16,128]{3,2,1,0:T(8,128)S(1)}, f32[2,4,16,128]{3,2,1,0:T(8,128)S(1)}, u32[]{:S(2)}, u32[]{:S(2)}) collective-permute-start(f32[2,4,16,128]{3,2,1,0:T(8,128)S(1)} %get-tuple-element.48), channel_id=1, source_target_pairs={{0,24},{8,0},{16,8},{24,16},{1,25},{9,1},{17,9},{25,17},{2,26},{10... | collective-permute-start | bytes 196616 | tf_op jit(solution)/shard_map/ppermute | solution.py:484
  31.2 2.7 %collective-permute-start.5 = (f32[2,8,16,128]{3,2,1,0:T(8,128)S(1)}, f32[2,8,16,128]{3,2,1,0:T(8,128)S(1)}, u32[]{:S(2)}, u32[]{:S(2)}) collective-permute-start(f32[2,8,16,128]{3,2,1,0:T(8,128)S(1)} %get-tuple-element.53), channel_id=1, source_target_pairs={{32,0},{64,32},{96,64},{128,96},{160,128},{192,160},{224,192},{256... | collective-permute-start | bytes 393224 | tf_op jit(solution)/shard_map/ppermute | solution.py:484
  34.0 1.9 %collective-permute-start = (f32[3,4,16,128]{3,2,1,0:T(8,128)S(1)}, f32[3,4,16,128]{3,2,1,0:T(8,128)S(1)}, u32[]{:S(2)}, u32[]{:S(2)}) collective-permute-start(f32[3,4,16,128]{3,2,1,0:T(8,128)S(1)} %get-tuple-element.47), channel_id=1, source_target_pairs={{0,8},{8,16},{16,24},{24,0},{1,9},{9,17},{17,25},{25,1},{2,10},{10... | collective-permute-start | bytes 294920 | tf_op jit(solution)/shard_map/ppermute | solution.py:484
  35.9 1.1 %collective-permute-start.2 = (f32[5,4,8,128]{3,2,1,0:T(8,128)S(1)}, f32[5,4,8,128]{3,2,1,0:T(8,128)S(1)}, u32[]{:S(2)}, u32[]{:S(2)}) collective-permute-start(f32[5,4,8,128]{3,2,1,0:T(8,128)S(1)} %get-tuple-element.49), channel_id=1, source_target_pairs={{0,1},{1,2},{2,3},{3,4},{4,5},{5,6},{6,7},{7,0},{8,9},{9,10},{10,1... | collective-permute-start | bytes 245768 | tf_op jit(solution)/shard_map/ppermute | solution.py:484
  37.0 8.3 %collective-permute-done.1.ky_down = f32[2,4,16,128]{3,2,1,0:T(8,128)S(1)} collective-permute-done((f32[2,4,16,128]{3,2,1,0:T(8,128)S(1)}, f32[2,4,16,128]{3,2,1,0:T(8,128)S(1)}, u32[]{:S(2)}, u32[]{:S(2)}) %collective-permute-start.1) | collective-permute-done | bytes 65568 | tf_op jit(solution)/shard_map/ppermute | solution.py:484
  45.3 0.8 collective-permute-start.3
  46.1 4.1 %collective-permute-done.3.kz_down = f32[4,4,8,128]{3,2,1,0:T(8,128)S(1)} collective-permute-done((f32[4,4,8,128]{3,2,1,0:T(8,128)S(1)}, f32[4,4,8,128]{3,2,1,0:T(8,128)S(1)}, u32[]{:S(2)}, u32[]{:S(2)}) %collective-permute-start.3) | collective-permute-done | bytes 65568 | tf_op jit(solution)/shard_map/ppermute | solution.py:484
  50.2 0.7 copy-done.9
  50.9 5.5 %shard_map.106 = (f32[4,8,16,128]{3,2,1,0:T(8,128)S(1)}, f32[3,4,8,16,128]{4,3,2,1,0:T(8,128)S(1)}, f32[3,4,16,128]{3,2,1,0:T(8,128)S(1)}) custom-call(f32[3,4]{1,0:T(4,128)S(1)} %copy-done.9, f32[4,8,16,128]{3,2,1,0:T(8,128)S(1)} %get-tuple-element.42.u_p, f32[4,8,16,128]{3,2,1,0:T(8,128)S(1)} %get-tuple-element.43.code_p, ...), custom_call_target="tpu_custom_call" | custom-call | flops 16000000 | bytes 2834480 | tf_op jit(solution)/shard_map/pallas_call | solution.py:470
  56.5 0.2 shard_map.107
  56.7 0.3 shard_map.108
  56.9 2.4 %shard_map.110 = f32[32,4,128]{2,1,0:T(4,128)} custom-call(f32[4,8,16,128]{3,2,1,0:T(8,128)S(1)} %get-tuple-element.59.section, f32[3,8,16,128]{3,2,1,0:T(8,128)S(1)} %get-tuple-element.44.fields_p, s32[8,16,128]{2,1,0:T(8,128)S(1)} %get-tuple-element.45.shell_p, f32[3,4,8,16,128]{4,3,2,1,0:T(8,128)S(1)} %get-tuple-element.66.slopes, ...), custom_call_target="tpu_custom_call" | custom-call | flops 4000000 | bytes 1474560 | tf_op jit(solution)/shard_map/pallas_call | solution.py:470
  59.3 8.2 %all-to-all-start.1 = ((f32[32,4,128]{2,1,0:T(4,128)}), f32[32,4,128]{2,1,0:T(4,128)S(1)}, u32[]{:S(2)}, u32[]{:S(2)}) async-start(f32[32,4,128]{2,1,0:T(4,128)} %shard_map.110), calls=%async_computation.1 | async-start | bytes 131072 | tf_op jit(solution)/shard_map/all_to_all | solution.py:494
  67.6 5.3 %collective-permute-start.10 = (f32[2,8,16,128]{3,2,1,0:T(8,128)S(1)}, f32[2,8,16,128]{3,2,1,0:T(8,128)S(1)}, u32[]{:S(2)}, u32[]{:S(2)}) collective-permute-start(f32[2,8,16,128]{3,2,1,0:T(8,128)S(1)} %get-tuple-element.64), channel_id=1, source_target_pairs={{0,32},{32,64},{64,96},{96,128},{128,160},{160,192},{192,224},{224... | collective-permute-start | bytes 393224 | tf_op jit(solution)/shard_map/ppermute | solution.py:484
  72.9 4.8 %collective-permute-start.11 = (f32[2,8,16,128]{3,2,1,0:T(8,128)S(1)}, f32[2,8,16,128]{3,2,1,0:T(8,128)S(1)}, u32[]{:S(2)}, u32[]{:S(2)}) collective-permute-start(f32[2,8,16,128]{3,2,1,0:T(8,128)S(1)} %get-tuple-element.65), channel_id=1, source_target_pairs={{32,0},{64,32},{96,64},{128,96},{160,128},{192,160},{224,192},{256... | collective-permute-start | bytes 393224 | tf_op jit(solution)/shard_map/ppermute | solution.py:484
  77.7 3.1 %collective-permute-start.6 = (f32[4,16,128]{2,1,0:T(8,128)S(1)}, f32[4,16,128]{2,1,0:T(8,128)S(1)}, u32[]{:S(2)}, u32[]{:S(2)}) collective-permute-start(f32[4,16,128]{2,1,0:T(8,128)S(1)} %get-tuple-element.60), channel_id=1, source_target_pairs={{0,8},{8,16},{16,24},{24,0},{1,9},{9,17},{17,25},{25,1},{2,10},{10... | collective-permute-start | bytes 98312 | tf_op jit(solution)/shard_map/ppermute | solution.py:484
  80.8 4.0 %collective-permute-start.7 = (f32[4,16,128]{2,1,0:T(8,128)S(1)}, f32[4,16,128]{2,1,0:T(8,128)S(1)}, u32[]{:S(2)}, u32[]{:S(2)}) collective-permute-start(f32[4,16,128]{2,1,0:T(8,128)S(1)} %get-tuple-element.61), channel_id=1, source_target_pairs={{0,24},{8,0},{16,8},{24,16},{1,25},{9,1},{17,9},{25,17},{2,26},{10... | collective-permute-start | bytes 98312 | tf_op jit(solution)/shard_map/ppermute | solution.py:484
  84.8 1.4 %collective-permute-start.8 = (f32[2,4,8,128]{3,2,1,0:T(8,128)S(1)}, f32[2,4,8,128]{3,2,1,0:T(8,128)S(1)}, u32[]{:S(2)}, u32[]{:S(2)}) collective-permute-start(f32[2,4,8,128]{3,2,1,0:T(8,128)S(1)} %get-tuple-element.62), channel_id=1, source_target_pairs={{0,1},{1,2},{2,3},{3,4},{4,5},{5,6},{6,7},{7,0},{8,9},{9,10},{10,1... | collective-permute-start | bytes 98312 | tf_op jit(solution)/shard_map/ppermute | solution.py:484
  86.1 5.9 %collective-permute-done.6.ky_up = f32[4,16,128]{2,1,0:T(8,128)S(1)} collective-permute-done((f32[4,16,128]{2,1,0:T(8,128)S(1)}, f32[4,16,128]{2,1,0:T(8,128)S(1)}, u32[]{:S(2)}, u32[]{:S(2)}) %collective-permute-start.6) | collective-permute-done | bytes 32800 | tf_op jit(solution)/shard_map/ppermute | solution.py:484
  92.0 0.6 collective-permute-start.9
  92.6 4.0 %collective-permute-done.9.kz_down = f32[2,4,8,128]{3,2,1,0:T(8,128)S(1)} collective-permute-done((f32[2,4,8,128]{3,2,1,0:T(8,128)S(1)}, f32[2,4,8,128]{3,2,1,0:T(8,128)S(1)}, u32[]{:S(2)}, u32[]{:S(2)}) %collective-permute-start.9) | collective-permute-done | bytes 32800 | tf_op jit(solution)/shard_map/ppermute | solution.py:484
  96.6 2.3 %shard_map.109.partial = f32[4,8,16,128]{3,2,1,0:T(8,128)S(1)} custom-call(f32[3,4]{1,0:T(4,128)S(1)} %copy-done.9, f32[4,8,16,128]{3,2,1,0:T(8,128)S(1)} %get-tuple-element.59.section, f32[4,8,16,128]{3,2,1,0:T(8,128)S(1)} %get-tuple-element.42.u_p, f32[4,8,16,128]{3,2,1,0:T(8,128)S(1)} %get-tuple-element.43.code_p, ...), custom_call_target="tpu_custom_call" | custom-call | flops 8000000 | bytes 1556528 | tf_op jit(solution)/shard_map/pallas_call | solution.py:470
  98.9 1.2 %shard_map.111 = (f32[4,16,16,64]{3,2,1,0:T(8,128)}, f32[3,4]{1,0:T(4,128)}) custom-call(f32[4,8,16,128]{3,2,1,0:T(8,128)S(1)} %shard_map.109.partial, f32[4,8,16,128]{3,2,1,0:T(8,128)S(1)} %get-tuple-element.59.section, f32[4,8,16,128]{3,2,1,0:T(8,128)S(1)} %get-tuple-element.43.code_p, f32[3,8,16,128]{3,2,1,0:T(8,128)S(1)} %get-tuple-element.44.fields_p, ...), custom_call_target="tpu_custom_call" | custom-call | flops 3000000 | bytes 1835056 | tf_op jit(solution)/shard_map/pallas_call | solution.py:470
  (24 shorter events, 0.2 us)
Async XLA Ops:
  0.6 1.0 %copy-start = (f32[4,16,16,64]{3,2,1,0:T(8,128)S(1)}, f32[4,16,16,64]{3,2,1,0:T(8,128)}, u32[]{:S(2)}) copy-start(f32[4,16,16,64]{3,2,1,0:T(8,128)} %u_ref.2) | copy-start | bytes 786436
  1.7 1.0 %copy-start.1 = (s32[4,16,16,64]{3,2,1,0:T(8,128)S(1)}, s32[4,16,16,64]{3,2,1,0:T(8,128)}, u32[]{:S(2)}) copy-start(s32[4,16,16,64]{3,2,1,0:T(8,128)} %code_ref.3) | copy-start | bytes 786436
  2.7 1.0 %copy-start.2 = (f32[4,16,16,64]{3,2,1,0:T(8,128)S(1)}, f32[4,16,16,64]{3,2,1,0:T(8,128)}, u32[]{:S(2)}) copy-start(f32[4,16,16,64]{3,2,1,0:T(8,128)} %start_ref.3) | copy-start | bytes 786436
  3.8 0.9 copy-start.5
  4.7 0.9 copy-start.6
  4.7 1.0 copy-start.7
  4.7 1.0 %copy-start.8 = (f32[16,16,64]{2,1,0:T(8,128)S(1)}, f32[16,16,64]{2,1,0:T(8,128)}, u32[]{:S(2)}) copy-start(f32[16,16,64]{2,1,0:T(8,128)} %in_ref.1) | copy-start | bytes 196612
  5.7 44.5 %copy-start.3 = (f32[4,16,16,64]{3,2,1,0:T(8,128)S(1)}, f32[4,16,16,64]{3,2,1,0:T(8,128)}, u32[]{:S(2)}) copy-start(f32[4,16,16,64]{3,2,1,0:T(8,128)} %start_ref.3) | copy-start | bytes 786436
  5.7 44.5 %copy-start.4 = (f32[4,16,16,64]{3,2,1,0:T(8,128)S(1)}, f32[4,16,16,64]{3,2,1,0:T(8,128)}, u32[]{:S(2)}) copy-start(f32[4,16,16,64]{3,2,1,0:T(8,128)} %section_ref.1) | copy-start | bytes 786436
  8.1 42.1 %all-to-all-start = ((f32[32,4,128]{2,1,0:T(4,128)}), f32[32,4,128]{2,1,0:T(4,128)S(1)}, u32[]{:S(2)}, u32[]{:S(2)}) async-start(f32[32,4,128]{2,1,0:T(4,128)} %get-tuple-element.46), calls=%async_computation | async-start | bytes 131072 | tf_op jit(solution)/shard_map/all_to_all | solution.py:494
  17.4 39.1 %collective-permute-start.4 = (f32[3,8,16,128]{3,2,1,0:T(8,128)S(1)}, f32[3,8,16,128]{3,2,1,0:T(8,128)S(1)}, u32[]{:S(2)}, u32[]{:S(2)}) collective-permute-start(f32[3,8,16,128]{3,2,1,0:T(8,128)S(1)} %get-tuple-element.52), channel_id=1, source_target_pairs={{0,32},{32,64},{64,96},{96,128},{128,160},{160,192},{192,224},{224... | collective-permute-start | bytes 589832 | tf_op jit(solution)/shard_map/ppermute | solution.py:484
  26.2 19.1 %collective-permute-start.1 = (f32[2,4,16,128]{3,2,1,0:T(8,128)S(1)}, f32[2,4,16,128]{3,2,1,0:T(8,128)S(1)}, u32[]{:S(2)}, u32[]{:S(2)}) collective-permute-start(f32[2,4,16,128]{3,2,1,0:T(8,128)S(1)} %get-tuple-element.48), channel_id=1, source_target_pairs={{0,24},{8,0},{16,8},{24,16},{1,25},{9,1},{17,9},{25,17},{2,26},{10... | collective-permute-start | bytes 196616 | tf_op jit(solution)/shard_map/ppermute | solution.py:484
  31.2 25.2 %collective-permute-start.5 = (f32[2,8,16,128]{3,2,1,0:T(8,128)S(1)}, f32[2,8,16,128]{3,2,1,0:T(8,128)S(1)}, u32[]{:S(2)}, u32[]{:S(2)}) collective-permute-start(f32[2,8,16,128]{3,2,1,0:T(8,128)S(1)} %get-tuple-element.53), channel_id=1, source_target_pairs={{32,0},{64,32},{96,64},{128,96},{160,128},{192,160},{224,192},{256... | collective-permute-start | bytes 393224 | tf_op jit(solution)/shard_map/ppermute | solution.py:484
  34.0 16.2 %collective-permute-start = (f32[3,4,16,128]{3,2,1,0:T(8,128)S(1)}, f32[3,4,16,128]{3,2,1,0:T(8,128)S(1)}, u32[]{:S(2)}, u32[]{:S(2)}) collective-permute-start(f32[3,4,16,128]{3,2,1,0:T(8,128)S(1)} %get-tuple-element.47), channel_id=1, source_target_pairs={{0,8},{8,16},{16,24},{24,0},{1,9},{9,17},{17,25},{25,1},{2,10},{10... | collective-permute-start | bytes 294920 | tf_op jit(solution)/shard_map/ppermute | solution.py:484
  35.9 14.3 %collective-permute-start.2 = (f32[5,4,8,128]{3,2,1,0:T(8,128)S(1)}, f32[5,4,8,128]{3,2,1,0:T(8,128)S(1)}, u32[]{:S(2)}, u32[]{:S(2)}) collective-permute-start(f32[5,4,8,128]{3,2,1,0:T(8,128)S(1)} %get-tuple-element.49), channel_id=1, source_target_pairs={{0,1},{1,2},{2,3},{3,4},{4,5},{5,6},{6,7},{7,0},{8,9},{9,10},{10,1... | collective-permute-start | bytes 245768 | tf_op jit(solution)/shard_map/ppermute | solution.py:484
  45.3 4.9 %collective-permute-start.3 = (f32[4,4,8,128]{3,2,1,0:T(8,128)S(1)}, f32[4,4,8,128]{3,2,1,0:T(8,128)S(1)}, u32[]{:S(2)}, u32[]{:S(2)}) collective-permute-start(f32[4,4,8,128]{3,2,1,0:T(8,128)S(1)} %get-tuple-element.50), channel_id=1, source_target_pairs={{0,7},{1,0},{2,1},{3,2},{4,3},{5,4},{6,5},{7,6},{8,15},{9,8},{10,9... | collective-permute-start | bytes 196616 | tf_op jit(solution)/shard_map/ppermute | solution.py:484
  50.2 0.7 copy-start.9
  59.3 39.6 %all-to-all-start.1 = ((f32[32,4,128]{2,1,0:T(4,128)}), f32[32,4,128]{2,1,0:T(4,128)S(1)}, u32[]{:S(2)}, u32[]{:S(2)}) async-start(f32[32,4,128]{2,1,0:T(4,128)} %shard_map.110), calls=%async_computation.1 | async-start | bytes 131072 | tf_op jit(solution)/shard_map/all_to_all | solution.py:494
  67.6 31.3 %collective-permute-start.10 = (f32[2,8,16,128]{3,2,1,0:T(8,128)S(1)}, f32[2,8,16,128]{3,2,1,0:T(8,128)S(1)}, u32[]{:S(2)}, u32[]{:S(2)}) collective-permute-start(f32[2,8,16,128]{3,2,1,0:T(8,128)S(1)} %get-tuple-element.64), channel_id=1, source_target_pairs={{0,32},{32,64},{64,96},{96,128},{128,160},{160,192},{192,224},{224... | collective-permute-start | bytes 393224 | tf_op jit(solution)/shard_map/ppermute | solution.py:484
  72.9 26.0 %collective-permute-start.11 = (f32[2,8,16,128]{3,2,1,0:T(8,128)S(1)}, f32[2,8,16,128]{3,2,1,0:T(8,128)S(1)}, u32[]{:S(2)}, u32[]{:S(2)}) collective-permute-start(f32[2,8,16,128]{3,2,1,0:T(8,128)S(1)} %get-tuple-element.65), channel_id=1, source_target_pairs={{32,0},{64,32},{96,64},{128,96},{160,128},{192,160},{224,192},{256... | collective-permute-start | bytes 393224 | tf_op jit(solution)/shard_map/ppermute | solution.py:484
  77.7 14.4 %collective-permute-start.6 = (f32[4,16,128]{2,1,0:T(8,128)S(1)}, f32[4,16,128]{2,1,0:T(8,128)S(1)}, u32[]{:S(2)}, u32[]{:S(2)}) collective-permute-start(f32[4,16,128]{2,1,0:T(8,128)S(1)} %get-tuple-element.60), channel_id=1, source_target_pairs={{0,8},{8,16},{16,24},{24,0},{1,9},{9,17},{17,25},{25,1},{2,10},{10... | collective-permute-start | bytes 98312 | tf_op jit(solution)/shard_map/ppermute | solution.py:484
  80.8 11.8 %collective-permute-start.7 = (f32[4,16,128]{2,1,0:T(8,128)S(1)}, f32[4,16,128]{2,1,0:T(8,128)S(1)}, u32[]{:S(2)}, u32[]{:S(2)}) collective-permute-start(f32[4,16,128]{2,1,0:T(8,128)S(1)} %get-tuple-element.61), channel_id=1, source_target_pairs={{0,24},{8,0},{16,8},{24,16},{1,25},{9,1},{17,9},{25,17},{2,26},{10... | collective-permute-start | bytes 98312 | tf_op jit(solution)/shard_map/ppermute | solution.py:484
  84.8 7.9 %collective-permute-start.8 = (f32[2,4,8,128]{3,2,1,0:T(8,128)S(1)}, f32[2,4,8,128]{3,2,1,0:T(8,128)S(1)}, u32[]{:S(2)}, u32[]{:S(2)}) collective-permute-start(f32[2,4,8,128]{3,2,1,0:T(8,128)S(1)} %get-tuple-element.62), channel_id=1, source_target_pairs={{0,1},{1,2},{2,3},{3,4},{4,5},{5,6},{6,7},{7,0},{8,9},{9,10},{10,1... | collective-permute-start | bytes 98312 | tf_op jit(solution)/shard_map/ppermute | solution.py:484
  92.0 4.6 %collective-permute-start.9 = (f32[2,4,8,128]{3,2,1,0:T(8,128)S(1)}, f32[2,4,8,128]{3,2,1,0:T(8,128)S(1)}, u32[]{:S(2)}, u32[]{:S(2)}) collective-permute-start(f32[2,4,8,128]{3,2,1,0:T(8,128)S(1)} %get-tuple-element.63), channel_id=1, source_target_pairs={{0,7},{1,0},{2,1},{3,2},{4,3},{5,4},{6,5},{7,6},{8,15},{9,8},{10,9... | collective-permute-start | bytes 98312 | tf_op jit(solution)/shard_map/ppermute | solution.py:484

commit v3 on v2

--- a/solution.py
+++ b/solution.py
@@ -207,7 +207,17 @@
     w_ref[r, (X + x) * Z : (X + x + 1) * Z, :] = value - head
 
 
-def edges_kernel(u_ref, code_ref, start_ref, vel_ref, pos_up, pos_down, ky_up, ky_down, kz_up, kz_down):
+def edges_kernel(
+    u_hbm, code_hbm, start_hbm, vel_hbm, pos_up, pos_down, ky_up, ky_down, kz_up, kz_down,
+    u_ref, code_ref, start_ref, vel_ref, arrived,
+):
+    pairs = ((u_hbm, u_ref), (code_hbm, code_ref), (vel_hbm, vel_ref), (start_hbm, start_ref))
+    copies = [pltpu.make_async_copy(a, b, arrived.at[n]) for n, (a, b) in enumerate(pairs)]
+    for copy in copies:
+        copy.start()
+    for copy in copies[:3]:
+        copy.wait()
+
     def whole(ref, x, r):
         return pack(ref[x, r], ref[x, r + R])
 
@@ -224,6 +234,7 @@
         pos_up[2, r] = c_far(d2) * (u2 - u3)
         pos_down[0, r] = u0
         pos_down[1, r] = c_low(d0) * (u0 - u1)
+    copies[3].wait()
     for x in range(X):
         k = 2 * R - 1
         d_last = digits_of(code_ref[x, k].astype(F32))[1]
@@ -252,7 +263,13 @@
         kz_down[3, x] = plane(start_ref, x, 1)
 
 
-def first_sums_kernel(u_ref, code_ref, vel_ref, shell_ref, out_ref, in_ref, u_p, code_p, fields_p, shell_p, sums, w_ref):
+def first_sums_kernel(
+    field, u_ref, code_ref, vel_ref, shell_ref, out_ref, in_ref, section_ref, start_ref,
+    u_p, code_p, fields_p, shell_p, field_p, section_p, start_p, sums, w_ref,
+):
+    for c in range(3):
+        for x in range(X):
+            field_p[c, x] = jnp.broadcast_to(field[c : c + 1, x : x + 1], (R, L))
     for r in range(R):
         fields_p[0, r] = pack(vel_ref[r], vel_ref[r + R])
         weight = pack(out_ref[r], out_ref[r + R])
@@ -263,6 +280,8 @@
             u = pack(u_ref[x, r], u_ref[x, r + R])
             u_p[x, r] = u
             code_p[x, r] = pack(code_ref[x, r], code_ref[x, r + R]).astype(F32)
+            section_p[x, r] = pack(section_ref[x, r], section_ref[x, r + R])
+            start_p[x, r] = pack(start_ref[x, r], start_ref[x, r + R])
             put_weighted(w_ref, r, x, weight * u)
     totals = shell_sums(w_ref, shell_p)
     tile = jnp.concatenate([totals, jnp.zeros_like(totals)], axis=1)
@@ -279,7 +298,7 @@
 
 def momentum_terms(sh, field, x, u, digit, k_ky, kz_rows):
     ks = (along_kx(sh, u, digit[3]), k_ky, along_kz(sh, u, digit[2], *kz_rows))
-    return ks, field[0, x] * ks[0] + field[1, x] * ks[1] + field[2, x] * ks[2]
+    return ks, sum(field[c, x, 0:1, :] * ks[c] for c in range(3))
 
 
 def face(digit, f_prev, f, f_next, f_next2):
@@ -288,17 +307,16 @@
 
 
 def section_kernel(
-    field, u_p, code_p, fields_p, shell_p, section_ref, start_ref, got_sums,
+    field, u_p, code_p, fields_p, section_p, start_p,
     ky_up, ky_down, kz_up, kz_down,
-    partial, slopes, grads,
+    partial, slopes,
 ):
     sh = Shifts()
-    totals = add_copies(got_sums)
 
     def body(x, carry):
         rows = [u_p[x, r] for r in range(R)]
         digit = [digits_of(code_p[x, r]) for r in range(R)]
-        start = [pack(start_ref[x, r], start_ref[x, r + R]) for r in range(R)]
+        start = [start_p[x, r] for r in range(R)]
         d_b, below = ky_up_rows(ky_up[0, x])
         s_below, f_below = ky_up_rows(ky_up[1, x])
         f_below2 = ky_up[2, x]
@@ -319,8 +337,7 @@
             up = [kz_up[n, x, r : r + 1, :] for n in range(5)]
             down = [kz_down[n, x, r : r + 1, :] for n in range(4)]
             ks, push = momentum_terms(sh, field, x, u, d, k_ky[r], (down[0], down[1], up[0], up[1], up[2]))
-            sec = pack(section_ref[x, r], section_ref[x, r + R])
-            grad_x = [g + sec * k for g, k in zip(grad_x, ks)]
+            grad_x = [g + section_p[x, r] * k for g, k in zip(grad_x, ks)]
             partial[x, r] = push
             faces_kx = face(d[3], sh.kx(f, 1), f, sh.kx(f, -1), sh.kx(f, -2))
             slopes[0, x, r] = faces_kx - sh.kx(faces_kx, 1)
@@ -330,33 +347,36 @@
             )
             slopes[2, x, r] = faces_kz - sh.kz_prev(faces_kz, face(up[0], up[4], up[3], f[0:1], f[1:2]))
         for c in range(3):
-            grads[c, x] = grad_x[c]
+            slopes[c, x, R] = grad_x[c]
         return carry
 
     lax.fori_loop(0, X, body, 0)
 
     def finish(r, carry):
-        v, back, shell = fields_p[0, r], fields_p[2, r], shell_p[r]
+        v = fields_p[0, r]
         us = [u_p[x, r] for x in range(X)]
         k_pos = pos_terms([v * u for u in us], [split6(code_p[x, r])[1] for x in range(X)])
         for x in range(X):
-            applied = back * gather(totals[x : x + 1], shell) - partial[x, r] - k_pos[x] - us[x]
-            partial[x, r] = 0.5 * us[x] + (0.5 * time_step) * applied
+            partial[x, r] = 0.5 * us[x] - (0.5 * time_step) * (partial[x, r] + k_pos[x] + us[x])
         return carry
 
     lax.fori_loop(0, R, finish, 0)
 
 
-def section_edges_kernel(partial, u_p, code_p, fields_p, got_up, got_down, section, pos_up, pos_down):
+def section_edges_kernel(
+    partial, u_p, code_p, fields_p, shell_p, got_up, got_down, got_sums, section, pos_up, pos_down
+):
+    totals = add_copies(got_sums)
+
     def body(r, carry):
-        v = fields_p[0, r]
+        v, back, shell = fields_p[0, r], fields_p[2, r], shell_p[r]
         d0, d2, d3 = (split6(code_p[x, r])[1] for x in (0, 2, 3))
         more = pos_corrections(
             v * u_p[0, r], d3, got_up[0, r], got_up[1, r], got_up[2, r], got_down[0, r], got_down[1, r]
         )
         m = []
         for x in range(X):
-            value = partial[x, r] - (0.5 * time_step) * more[x]
+            value = partial[x, r] + (0.5 * time_step) * (back * gather(totals[x : x + 1], shell) - more[x])
             section[x, r] = value
             m.append(v * value)
         pos_up[0, r] = m[3]
@@ -385,12 +405,12 @@
         kz_down[1, x] = c_low(digits_of(code_p[x, :, 0, :])[2]) * (first - second)
 
 
-def second_sums_kernel(section, fields_p, shell_p, slopes, grads, sums, w_ref):
+def second_sums_kernel(section, fields_p, shell_p, slopes, sums, w_ref):
     row = lax.broadcasted_iota(jnp.int32, (X, SHELLS), 0)
     column = lax.broadcasted_iota(jnp.int32, (X, SHELLS), 1)
     inner = jnp.zeros((X, SHELLS), F32)
     for x in range(X):
-        parts = [(0.5 * time_step) * grads[c, x] for c in range(3)]
+        parts = [(0.5 * time_step) * slopes[c, x, R] for c in range(3)]
         for r in range(R):
             value = section[x, r]
             put_weighted(w_ref, r, x, fields_p[1, r] * value)
@@ -462,17 +482,20 @@
         grad[c : c + 1, :] = line[:, :X] * scale
 
 
-def call(kernel, outs, args, scalars=0, scratch=(), ops=0):
+def call(kernel, outs, args, in_hbm=False, scratch=(), ops=0, aliases={}):
+    if in_hbm:
+        args = [pltpu.with_memory_space_constraint(a, pltpu.HBM) for a in args]
     shapes = [jax.ShapeDtypeStruct(shape, F32 if dtype is None else dtype) for shape, dtype in outs]
     moved = sum(4 * a.size for a in args) + sum(4 * s.size for s in shapes)
     vmem = pl.BlockSpec(memory_space=pltpu.VMEM)
-    smem = pl.BlockSpec(memory_space=pltpu.SMEM)
+    given = pl.BlockSpec(memory_space=pltpu.HBM) if in_hbm else vmem
     return pl.pallas_call(
         kernel,
         out_shape=shapes,
-        in_specs=[smem] * scalars + [vmem] * (len(args) - scalars),
+        in_specs=[given] * len(args),
         out_specs=[vmem] * len(shapes),
         scratch_shapes=list(scratch),
+        input_output_aliases=aliases,
         compiler_params=pltpu.CompilerParams(vmem_limit_bytes=VMEM_LIMIT),
         cost_estimate=pl.CostEstimate(flops=ops, bytes_accessed=moved, transcendentals=0),
     )(*args)
@@ -509,38 +532,39 @@
     plane, ky_plane, kz_plane = (R, Z, L), (X, Z, L), (X, R, L)
     w_scratch = [pltpu.VMEM((R, 2 * X * Z, L), F32)]
     sums_shape = ((members, X, L), None)
-    up, down, ky_up, ky_down, kz_up, kz_down = call(
+    up, down, ky_up, ky_down, kz_up, kz_down, u_v, code_v, start_v, vel_v = call(
         edges_kernel,
         [((3,) + plane, None), ((2,) + plane, None), ((3,) + ky_plane, None), ((2,) + ky_plane, None),
-         ((5,) + kz_plane, None), ((4,) + kz_plane, None)],
+         ((5,) + kz_plane, None), ((4,) + kz_plane, None), (cotangent.shape, None), (cotangent.shape, jnp.int32),
+         (cotangent.shape, None), (velocity.shape, None)],
         [cotangent, face_codes, start_state, velocity],
+        in_hbm=True,
+        scratch=[pltpu.SemaphoreType.DMA((4,))],
         ops=4_000_000,
-    )
-    cotangent, up, down, ky_up, ky_down, kz_up, kz_down = lax.optimization_barrier(
-        (cotangent, up, down, ky_up, ky_down, kz_up, kz_down)
     )
     up, down = shift_both(up, down, "pos", False)
     ky_up, ky_down = shift_both(ky_up, ky_down, "ky")
     kz_up, kz_down = shift_both(kz_up, kz_down, "kz")
-    u_p, code_p, fields_p, shell_p, sums = call(
+    u_p, code_p, fields_p, shell_p, field_p, section_p, start_p, sums = call(
         first_sums_kernel,
-        [(FULL, None), (FULL, None), ((3,) + plane, None), (plane, jnp.int32), sums_shape],
-        [cotangent, face_codes, velocity, shell_index, shell_out, shell_in],
+        [(FULL, None), (FULL, None), ((3,) + plane, None), (plane, jnp.int32), ((3, X, R, L), None),
+         (FULL, None), (FULL, None), sums_shape],
+        [field_strength, u_v, code_v, vel_v, shell_index, shell_out, shell_in, section_state, start_v],
         scratch=w_scratch,
         ops=8_000_000,
     )
     sums = exchange(sums)
-    partial, slopes, grads = call(
+    partial, slopes = call(
         section_kernel,
-        [(FULL, None), ((3,) + FULL, None), ((3, X, Z, L), None)],
-        [field_strength, u_p, code_p, fields_p, shell_p, section_state, start_state, sums, ky_up, ky_down, kz_up, kz_down],
-        scalars=1,
+        [(FULL, None), ((3, X, R + 1, Z, L), None)],
+        [field_p, u_p, code_p, fields_p, section_p, start_p, ky_up, ky_down, kz_up, kz_down],
         ops=16_000_000,
     )
     section, up2, down2 = call(
         section_edges_kernel,
         [(FULL, None), ((2,) + plane, None), ((2,) + plane, None)],
-        [partial, u_p, code_p, fields_p, up, down],
+        [partial, u_p, code_p, fields_p, shell_p, up, down, sums],
+        aliases={0: 0},
         ops=2_000_000,
     )
     up2, down2 = shift_both(up2, down2, "pos", False)
@@ -550,20 +574,16 @@
         [section, code_p],
         ops=1_000_000,
     )
-    section, ky_up2, ky_down2, kz_up2, kz_down2 = lax.optimization_barrier(
-        (section, ky_up2, ky_down2, kz_up2, kz_down2)
-    )
     ky_up2, ky_down2 = shift_both(ky_up2, ky_down2, "ky")
     kz_up2, kz_down2 = shift_both(kz_up2, kz_down2, "kz")
     (sums2,) = call(
-        second_sums_kernel, [sums_shape], [section, fields_p, shell_p, slopes, grads], scratch=w_scratch, ops=4_000_000
+        second_sums_kernel, [sums_shape], [section, fields_p, shell_p, slopes], scratch=w_scratch, ops=4_000_000
     )
     sums2 = exchange(sums2)
     (partial2,) = call(
         interior_kernel,
         [(FULL, None)],
-        [field_strength, section, u_p, code_p, fields_p, ky_up, kz_up, ky_up2, ky_down2, kz_up2, kz_down2],
-        scalars=1,
+        [field_p, section, u_p, code_p, fields_p, ky_up, kz_up, ky_up2, ky_down2, kz_up2, kz_down2],
         ops=8_000_000,
     )
     state_adjoint, field_grad = call(

time: 101 us -> 98.8 us (0.978)
  the two profiles are of different devices: /device:TPU:15 before, /device:TPU:23 now
where the time goes in v3:
time: 98.8 us; the launch traced here: 98.3 us
  starting transfers between devices  56.6 us (57%)
  waiting for transfers between devices  24.4 us (25%)
  Pallas kernels  15.8 us (16%)
    ppermute x12, starting transfers between devices, shift(): return lax.ppermute(array, axis, pairs)  39.3 us
    ppermute x12, waiting for transfers between devices, shift(): return lax.ppermute(array, axis, pairs)  24.4 us
    all_to_all x2, starting transfers between devices, exchange(): return lax.all_to_all(copies, ('ky', 'kz'), 0, 0)  17.3 us
    pallas_call x8, Pallas kernels, call(): pl.pallas_call(kernel, out_shape=shapes, in_specs=[given] * len(args), ou...  15.8 us
  transfers between devices with their start and end apart: 14, of which 4 were waited for; matrix products, arithmetic and copies ran while one was open for 0% of the time, Pallas kernels for 7%

profile of v3, /device:TPU:23, one launch (start us, length us, event | category | flops | bytes accessed | tf_op | source)
XLA Modules:
  0.0 98.3 jit_solution(801263373057875722)
XLA Ops:
  0.7 2.4 %shard_map.104 = (f32[3,8,16,128]{3,2,1,0:T(8,128)S(1)}, f32[2,8,16,128]{3,2,1,0:T(8,128)S(1)}, f32[3,4,16,128]{3,2,1,0:T(8,128)S(1)}, f32[2,4,16,128]{3,2,1,0:T...) custom-call(f32[4,16,16,64]{3,2,1,0:T(8,128)} %u_hbm.1, ...), custom_call_target="tpu_custom_call" | custom-call | flops 4000000 | bytes 2342912 | tf_op jit(solution)/shard_map/pallas_call | solution.py:492
  3.1 0.0 copy-start.4
  3.1 0.6 copy-done.4
  3.8 2.6 %shard_map.105 = (f32[4,8,16,128]{3,2,1,0:T(8,128)S(1)}, f32[4,8,16,128]{3,2,1,0:T(8,128)S(1)}, f32[3,8,16,128]{3,2,1,0:T(8,128)S(1)}, s32[8,16,128]{2,1,0:T(8,1...) custom-call(f32[3,4]{1,0:T(4,128)S(1)} %copy-done.4, ...), custom_call_target="tpu_custom_call" | custom-call | flops 8000000 | bytes 2736176 | tf_op jit(solution)/shard_map/pallas_call | solution.py:492
  6.3 9.3 %all-to-all-start = ((f32[32,4,128]{2,1,0:T(4,128)}), f32[32,4,128]{2,1,0:T(4,128)S(1)}, u32[]{:S(2)}, u32[]{:S(2)}) async-start(f32[32,4,128]{2,1,0:T(4,128)} %get-tuple-element.47), calls=%async_computation | async-start | bytes 131072 | tf_op jit(solution)/shard_map/all_to_all | solution.py:517
  15.6 8.8 %collective-permute-start.4 = (f32[3,8,16,128]{3,2,1,0:T(8,128)S(1)}, f32[3,8,16,128]{3,2,1,0:T(8,128)S(1)}, u32[]{:S(2)}, u32[]{:S(2)}) collective-permute-start(f32[3,8,16,128]{3,2,1,0:T(8,128)S(1)} %get-tuple-element.45), channel_id=1, source_target_pairs={{0,32},{32,64},{64,96},{96,128},{128,160},{160,192},{192,224},{224... | collective-permute-start | bytes 589832 | tf_op jit(solution)/shard_map/ppermute | solution.py:507
  24.4 5.0 %collective-permute-start.1 = (f32[2,4,16,128]{3,2,1,0:T(8,128)}, f32[2,4,16,128]{3,2,1,0:T(8,128)S(1)}, u32[]{:S(2)}, u32[]{:S(2)}) collective-permute-start(f32[2,4,16,128]{3,2,1,0:T(8,128)} %get-tuple-element.40), channel_id=1, source_target_pairs={{0,24},{8,0},{16,8},{24,16},{1,25},{9,1},{17,9},{25,17},{2,26},{10... | collective-permute-start | bytes 196616 | tf_op jit(solution)/shard_map/ppermute | solution.py:507
  29.4 2.7 %collective-permute-start.5 = (f32[2,8,16,128]{3,2,1,0:T(8,128)S(1)}, f32[2,8,16,128]{3,2,1,0:T(8,128)S(1)}, u32[]{:S(2)}, u32[]{:S(2)}) collective-permute-start(f32[2,8,16,128]{3,2,1,0:T(8,128)S(1)} %get-tuple-element.46), channel_id=1, source_target_pairs={{32,0},{64,32},{96,64},{128,96},{160,128},{192,160},{224,192},{256... | collective-permute-start | bytes 393224 | tf_op jit(solution)/shard_map/ppermute | solution.py:507
  32.2 1.9 %collective-permute-start = (f32[3,4,16,128]{3,2,1,0:T(8,128)S(1)}, f32[3,4,16,128]{3,2,1,0:T(8,128)S(1)}, u32[]{:S(2)}, u32[]{:S(2)}) collective-permute-start(f32[3,4,16,128]{3,2,1,0:T(8,128)S(1)} %get-tuple-element.39), channel_id=1, source_target_pairs={{0,8},{8,16},{16,24},{24,0},{1,9},{9,17},{17,25},{25,1},{2,10},{10... | collective-permute-start | bytes 294920 | tf_op jit(solution)/shard_map/ppermute | solution.py:507
  34.1 1.1 %collective-permute-start.2 = (f32[5,4,8,128]{3,2,1,0:T(8,128)S(1)}, f32[5,4,8,128]{3,2,1,0:T(8,128)S(1)}, u32[]{:S(2)}, u32[]{:S(2)}) collective-permute-start(f32[5,4,8,128]{3,2,1,0:T(8,128)S(1)} %get-tuple-element.41), channel_id=1, source_target_pairs={{0,1},{1,2},{2,3},{3,4},{4,5},{5,6},{6,7},{7,0},{8,9},{9,10},{10,1... | collective-permute-start | bytes 245768 | tf_op jit(solution)/shard_map/ppermute | solution.py:507
  35.2 8.8 %collective-permute-done.1.ky_down = f32[2,4,16,128]{3,2,1,0:T(8,128)S(1)} collective-permute-done((f32[2,4,16,128]{3,2,1,0:T(8,128)}, f32[2,4,16,128]{3,2,1,0:T(8,128)S(1)}, u32[]{:S(2)}, u32[]{:S(2)}) %collective-permute-start.1) | collective-permute-done | bytes 65568 | tf_op jit(solution)/shard_map/ppermute | solution.py:507
  43.9 0.6 collective-permute-start.3
  44.5 4.3 %collective-permute-done.3.kz_down = f32[4,4,8,128]{3,2,1,0:T(8,128)S(1)} collective-permute-done((f32[4,4,8,128]{3,2,1,0:T(8,128)S(1)}, f32[4,4,8,128]{3,2,1,0:T(8,128)S(1)}, u32[]{:S(2)}, u32[]{:S(2)}) %collective-permute-start.3) | collective-permute-done | bytes 65568 | tf_op jit(solution)/shard_map/ppermute | solution.py:507
  48.8 0.0 collective-permute-done.2.kz_up.first_kz
  48.8 0.0 collective-permute-done.ky_up.first_up
  48.8 4.5 %shard_map.106 = (f32[4,8,16,128]{3,2,1,0:T(8,128)S(1)}, f32[3,4,9,16,128]{4,3,2,1,0:T(8,128)S(1)}) custom-call(f32[3,4,8,128]{3,2,1,0:T(8,128)S(1)} %get-tuple-element.33.field, f32[4,8,16,128]{3,2,1,0:T(8,128)S(1)} %get-tuple-element.34.u_p, f32[4,8,16,128]{3,2,1,0:T(8,128)S(1)} %get-tuple-element.35.code_p, ...), custom_call_target="tpu_custom_call" | custom-call | flops 16000000 | bytes 2752512 | tf_op jit(solution)/shard_map/pallas_call | solution.py:492
  53.3 0.0 all-to-all-done.got_sums
  53.3 0.8 shard_map.107
  54.2 2.3 %shard_map.110 = f32[32,4,128]{2,1,0:T(4,128)} custom-call(f32[4,8,16,128]{3,2,1,0:T(8,128)S(1)} %get-tuple-element.48.section, f32[3,8,16,128]{3,2,1,0:T(8,128)S(1)} %get-tuple-element.36.fields_p, s32[8,16,128]{2,1,0:T(8,128)S(1)} %get-tuple-element.44.shell_p, f32[3,4,9,16,128]{4,3,2,1,0:T(8,128)S(1)} %get-tuple-element.55.slopes), custom_call_target="tpu_custom_call" | custom-call | flops 4000000 | bytes 1474560 | tf_op jit(solution)/shard_map/pallas_call | solution.py:492
  56.5 8.0 %all-to-all-start.1 = ((f32[32,4,128]{2,1,0:T(4,128)}), f32[32,4,128]{2,1,0:T(4,128)S(1)}, u32[]{:S(2)}, u32[]{:S(2)}) async-start(f32[32,4,128]{2,1,0:T(4,128)} %shard_map.110), calls=%async_computation.1 | async-start | bytes 131072 | tf_op jit(solution)/shard_map/all_to_all | solution.py:517
  64.5 5.9 %collective-permute-start.10 = (f32[2,8,16,128]{3,2,1,0:T(8,128)S(1)}, f32[2,8,16,128]{3,2,1,0:T(8,128)S(1)}, u32[]{:S(2)}, u32[]{:S(2)}) collective-permute-start(f32[2,8,16,128]{3,2,1,0:T(8,128)S(1)} %get-tuple-element.53), channel_id=1, source_target_pairs={{0,32},{32,64},{64,96},{96,128},{128,160},{160,192},{192,224},{224... | collective-permute-start | bytes 393224 | tf_op jit(solution)/shard_map/ppermute | solution.py:507
  70.4 4.2 %collective-permute-start.11 = (f32[2,8,16,128]{3,2,1,0:T(8,128)S(1)}, f32[2,8,16,128]{3,2,1,0:T(8,128)S(1)}, u32[]{:S(2)}, u32[]{:S(2)}) collective-permute-start(f32[2,8,16,128]{3,2,1,0:T(8,128)S(1)} %get-tuple-element.54), channel_id=1, source_target_pairs={{32,0},{64,32},{96,64},{128,96},{160,128},{192,160},{224,192},{256... | collective-permute-start | bytes 393224 | tf_op jit(solution)/shard_map/ppermute | solution.py:507
  74.6 0.3 shard_map.108
  74.9 3.1 %collective-permute-start.6 = (f32[4,16,128]{2,1,0:T(8,128)S(1)}, f32[4,16,128]{2,1,0:T(8,128)S(1)}, u32[]{:S(2)}, u32[]{:S(2)}) collective-permute-start(f32[4,16,128]{2,1,0:T(8,128)S(1)} %get-tuple-element.49), channel_id=1, source_target_pairs={{0,8},{8,16},{16,24},{24,0},{1,9},{9,17},{17,25},{25,1},{2,10},{10... | collective-permute-start | bytes 98312 | tf_op jit(solution)/shard_map/ppermute | solution.py:507
  78.0 4.0 %collective-permute-start.7 = (f32[4,16,128]{2,1,0:T(8,128)S(1)}, f32[4,16,128]{2,1,0:T(8,128)S(1)}, u32[]{:S(2)}, u32[]{:S(2)}) collective-permute-start(f32[4,16,128]{2,1,0:T(8,128)S(1)} %get-tuple-element.50), channel_id=1, source_target_pairs={{0,24},{8,0},{16,8},{24,16},{1,25},{9,1},{17,9},{25,17},{2,26},{10... | collective-permute-start | bytes 98312 | tf_op jit(solution)/shard_map/ppermute | solution.py:507
  82.0 1.4 %collective-permute-start.8 = (f32[2,4,8,128]{3,2,1,0:T(8,128)S(1)}, f32[2,4,8,128]{3,2,1,0:T(8,128)S(1)}, u32[]{:S(2)}, u32[]{:S(2)}) collective-permute-start(f32[2,4,8,128]{3,2,1,0:T(8,128)S(1)} %get-tuple-element.51), channel_id=1, source_target_pairs={{0,1},{1,2},{2,3},{3,4},{4,5},{5,6},{6,7},{7,0},{8,9},{9,10},{10,1... | collective-permute-start | bytes 98312 | tf_op jit(solution)/shard_map/ppermute | solution.py:507
  83.3 7.5 %collective-permute-done.6.ky_up = f32[4,16,128]{2,1,0:T(8,128)S(1)} collective-permute-done((f32[4,16,128]{2,1,0:T(8,128)S(1)}, f32[4,16,128]{2,1,0:T(8,128)S(1)}, u32[]{:S(2)}, u32[]{:S(2)}) %collective-permute-start.6) | collective-permute-done | bytes 32800 | tf_op jit(solution)/shard_map/ppermute | solution.py:507
  90.8 0.7 collective-permute-start.9
  91.5 0.0 collective-permute-done.8.kz_up
  91.5 3.9 %collective-permute-done.9.kz_down = f32[2,4,8,128]{3,2,1,0:T(8,128)S(1)} collective-permute-done((f32[2,4,8,128]{3,2,1,0:T(8,128)S(1)}, f32[2,4,8,128]{3,2,1,0:T(8,128)S(1)}, u32[]{:S(2)}, u32[]{:S(2)}) %collective-permute-start.9) | collective-permute-done | bytes 32800 | tf_op jit(solution)/shard_map/ppermute | solution.py:507
  95.4 1.7 %shard_map.109.partial = f32[4,8,16,128]{3,2,1,0:T(8,128)S(1)} custom-call(f32[3,4,8,128]{3,2,1,0:T(8,128)S(1)} %get-tuple-element.33.field, f32[4,8,16,128]{3,2,1,0:T(8,128)S(1)} %get-tuple-element.48.section, f32[4,8,16,128]{3,2,1,0:T(8,128)S(1)} %get-tuple-element.34.u_p, f32[4,8,16,128]{3,2,1,0:T(8,128)S(1)} %get-tuple-element.35.code_p, ...), custom_call_target="tpu_custom_call" | custom-call | flops 8000000 | bytes 1605632 | tf_op jit(solution)/shard_map/pallas_call | solution.py:492
  97.1 1.2 %shard_map.111 = (f32[4,16,16,64]{3,2,1,0:T(8,128)}, f32[3,4]{1,0:T(4,128)}) custom-call(f32[4,8,16,128]{3,2,1,0:T(8,128)S(1)} %shard_map.109.partial, f32[4,8,16,128]{3,2,1,0:T(8,128)S(1)} %get-tuple-element.48.section, f32[4,8,16,128]{3,2,1,0:T(8,128)S(1)} %get-tuple-element.35.code_p, f32[3,8,16,128]{3,2,1,0:T(8,128)S(1)} %get-tuple-element.36.fields_p, ...), custom_call_target="tpu_custom_call" | custom-call | flops 3000000 | bytes 1835056 | tf_op jit(solution)/shard_map/pallas_call | solution.py:492
  (14 shorter events, 0.0 us)
Async XLA Ops:
  0.6 2.4 %copy-start.3 = (f32[16,16,64]{2,1,0:T(8,128)S(1)}, f32[16,16,64]{2,1,0:T(8,128)}, u32[]{:S(2)}) copy-start(f32[16,16,64]{2,1,0:T(8,128)} %in_ref.1) | copy-start | bytes 196612
  0.6 2.4 %copy-start.2 = (f32[16,16,64]{2,1,0:T(8,128)S(1)}, f32[16,16,64]{2,1,0:T(8,128)}, u32[]{:S(2)}) copy-start(f32[16,16,64]{2,1,0:T(8,128)} %out_ref.1) | copy-start | bytes 196612
  0.7 2.4 %copy-start.1 = (s32[16,16,64]{2,1,0:T(8,128)S(1)}, s32[16,16,64]{2,1,0:T(8,128)}, u32[]{:S(2)}) copy-start(s32[16,16,64]{2,1,0:T(8,128)} %shell_ref.1) | copy-start | bytes 196612
  0.7 2.4 %copy-start = (f32[4,16,16,64]{3,2,1,0:T(8,128)S(1)}, f32[4,16,16,64]{3,2,1,0:T(8,128)}, u32[]{:S(2)}) copy-start(f32[4,16,16,64]{3,2,1,0:T(8,128)} %section_ref.1) | copy-start | bytes 786436
  3.1 0.7 copy-start.4
  6.3 47.0 %all-to-all-start = ((f32[32,4,128]{2,1,0:T(4,128)}), f32[32,4,128]{2,1,0:T(4,128)S(1)}, u32[]{:S(2)}, u32[]{:S(2)}) async-start(f32[32,4,128]{2,1,0:T(4,128)} %get-tuple-element.47), calls=%async_computation | async-start | bytes 131072 | tf_op jit(solution)/shard_map/all_to_all | solution.py:517
  15.6 37.7 %collective-permute-start.4 = (f32[3,8,16,128]{3,2,1,0:T(8,128)S(1)}, f32[3,8,16,128]{3,2,1,0:T(8,128)S(1)}, u32[]{:S(2)}, u32[]{:S(2)}) collective-permute-start(f32[3,8,16,128]{3,2,1,0:T(8,128)S(1)} %get-tuple-element.45), channel_id=1, source_target_pairs={{0,32},{32,64},{64,96},{96,128},{128,160},{160,192},{192,224},{224... | collective-permute-start | bytes 589832 | tf_op jit(solution)/shard_map/ppermute | solution.py:507
  24.4 19.5 %collective-permute-start.1 = (f32[2,4,16,128]{3,2,1,0:T(8,128)}, f32[2,4,16,128]{3,2,1,0:T(8,128)S(1)}, u32[]{:S(2)}, u32[]{:S(2)}) collective-permute-start(f32[2,4,16,128]{3,2,1,0:T(8,128)} %get-tuple-element.40), channel_id=1, source_target_pairs={{0,24},{8,0},{16,8},{24,16},{1,25},{9,1},{17,9},{25,17},{2,26},{10... | collective-permute-start | bytes 196616 | tf_op jit(solution)/shard_map/ppermute | solution.py:507
  29.4 23.9 %collective-permute-start.5 = (f32[2,8,16,128]{3,2,1,0:T(8,128)S(1)}, f32[2,8,16,128]{3,2,1,0:T(8,128)S(1)}, u32[]{:S(2)}, u32[]{:S(2)}) collective-permute-start(f32[2,8,16,128]{3,2,1,0:T(8,128)S(1)} %get-tuple-element.46), channel_id=1, source_target_pairs={{32,0},{64,32},{96,64},{128,96},{160,128},{192,160},{224,192},{256... | collective-permute-start | bytes 393224 | tf_op jit(solution)/shard_map/ppermute | solution.py:507
  32.2 16.7 %collective-permute-start = (f32[3,4,16,128]{3,2,1,0:T(8,128)S(1)}, f32[3,4,16,128]{3,2,1,0:T(8,128)S(1)}, u32[]{:S(2)}, u32[]{:S(2)}) collective-permute-start(f32[3,4,16,128]{3,2,1,0:T(8,128)S(1)} %get-tuple-element.39), channel_id=1, source_target_pairs={{0,8},{8,16},{16,24},{24,0},{1,9},{9,17},{17,25},{25,1},{2,10},{10... | collective-permute-start | bytes 294920 | tf_op jit(solution)/shard_map/ppermute | solution.py:507
  34.1 14.7 %collective-permute-start.2 = (f32[5,4,8,128]{3,2,1,0:T(8,128)S(1)}, f32[5,4,8,128]{3,2,1,0:T(8,128)S(1)}, u32[]{:S(2)}, u32[]{:S(2)}) collective-permute-start(f32[5,4,8,128]{3,2,1,0:T(8,128)S(1)} %get-tuple-element.41), channel_id=1, source_target_pairs={{0,1},{1,2},{2,3},{3,4},{4,5},{5,6},{6,7},{7,0},{8,9},{9,10},{10,1... | collective-permute-start | bytes 245768 | tf_op jit(solution)/shard_map/ppermute | solution.py:507
  43.9 4.9 %collective-permute-start.3 = (f32[4,4,8,128]{3,2,1,0:T(8,128)S(1)}, f32[4,4,8,128]{3,2,1,0:T(8,128)S(1)}, u32[]{:S(2)}, u32[]{:S(2)}) collective-permute-start(f32[4,4,8,128]{3,2,1,0:T(8,128)S(1)} %get-tuple-element.42), channel_id=1, source_target_pairs={{0,7},{1,0},{2,1},{3,2},{4,3},{5,4},{6,5},{7,6},{8,15},{9,8},{10,9... | collective-permute-start | bytes 196616 | tf_op jit(solution)/shard_map/ppermute | solution.py:507
  56.5 40.6 %all-to-all-start.1 = ((f32[32,4,128]{2,1,0:T(4,128)}), f32[32,4,128]{2,1,0:T(4,128)S(1)}, u32[]{:S(2)}, u32[]{:S(2)}) async-start(f32[32,4,128]{2,1,0:T(4,128)} %shard_map.110), calls=%async_computation.1 | async-start | bytes 131072 | tf_op jit(solution)/shard_map/all_to_all | solution.py:517
  64.5 32.6 %collective-permute-start.10 = (f32[2,8,16,128]{3,2,1,0:T(8,128)S(1)}, f32[2,8,16,128]{3,2,1,0:T(8,128)S(1)}, u32[]{:S(2)}, u32[]{:S(2)}) collective-permute-start(f32[2,8,16,128]{3,2,1,0:T(8,128)S(1)} %get-tuple-element.53), channel_id=1, source_target_pairs={{0,32},{32,64},{64,96},{96,128},{128,160},{160,192},{192,224},{224... | collective-permute-start | bytes 393224 | tf_op jit(solution)/shard_map/ppermute | solution.py:507
  70.4 26.7 %collective-permute-start.11 = (f32[2,8,16,128]{3,2,1,0:T(8,128)S(1)}, f32[2,8,16,128]{3,2,1,0:T(8,128)S(1)}, u32[]{:S(2)}, u32[]{:S(2)}) collective-permute-start(f32[2,8,16,128]{3,2,1,0:T(8,128)S(1)} %get-tuple-element.54), channel_id=1, source_target_pairs={{32,0},{64,32},{96,64},{128,96},{160,128},{192,160},{224,192},{256... | collective-permute-start | bytes 393224 | tf_op jit(solution)/shard_map/ppermute | solution.py:507
  74.9 15.9 %collective-permute-start.6 = (f32[4,16,128]{2,1,0:T(8,128)S(1)}, f32[4,16,128]{2,1,0:T(8,128)S(1)}, u32[]{:S(2)}, u32[]{:S(2)}) collective-permute-start(f32[4,16,128]{2,1,0:T(8,128)S(1)} %get-tuple-element.49), channel_id=1, source_target_pairs={{0,8},{8,16},{16,24},{24,0},{1,9},{9,17},{17,25},{25,1},{2,10},{10... | collective-permute-start | bytes 98312 | tf_op jit(solution)/shard_map/ppermute | solution.py:507
  78.0 13.5 %collective-permute-start.7 = (f32[4,16,128]{2,1,0:T(8,128)S(1)}, f32[4,16,128]{2,1,0:T(8,128)S(1)}, u32[]{:S(2)}, u32[]{:S(2)}) collective-permute-start(f32[4,16,128]{2,1,0:T(8,128)S(1)} %get-tuple-element.50), channel_id=1, source_target_pairs={{0,24},{8,0},{16,8},{24,16},{1,25},{9,1},{17,9},{25,17},{2,26},{10... | collective-permute-start | bytes 98312 | tf_op jit(solution)/shard_map/ppermute | solution.py:507
  82.0 9.5 %collective-permute-start.8 = (f32[2,4,8,128]{3,2,1,0:T(8,128)S(1)}, f32[2,4,8,128]{3,2,1,0:T(8,128)S(1)}, u32[]{:S(2)}, u32[]{:S(2)}) collective-permute-start(f32[2,4,8,128]{3,2,1,0:T(8,128)S(1)} %get-tuple-element.51), channel_id=1, source_target_pairs={{0,1},{1,2},{2,3},{3,4},{4,5},{5,6},{6,7},{7,0},{8,9},{9,10},{10,1... | collective-permute-start | bytes 98312 | tf_op jit(solution)/shard_map/ppermute | solution.py:507
  90.8 4.6 %collective-permute-start.9 = (f32[2,4,8,128]{3,2,1,0:T(8,128)S(1)}, f32[2,4,8,128]{3,2,1,0:T(8,128)S(1)}, u32[]{:S(2)}, u32[]{:S(2)}) collective-permute-start(f32[2,4,8,128]{3,2,1,0:T(8,128)S(1)} %get-tuple-element.52), channel_id=1, source_target_pairs={{0,7},{1,0},{2,1},{3,2},{4,3},{5,4},{6,5},{7,6},{8,15},{9,8},{10,9... | collective-permute-start | bytes 98312 | tf_op jit(solution)/shard_map/ppermute | solution.py:507

commit v4 on v3

--- a/solution.py
+++ b/solution.py
@@ -77,21 +77,13 @@
     def __init__(self):
         lane = lanes((Z, L))
         self.low = lane < HALF
-        kx = lane & (HALF - 1)
-        self.kx_first, self.kx_second = kx == 0, kx < 2
-        self.kx_last, self.kx_pair = kx == HALF - 1, kx >= HALF - 2
+        self.moved = {by: (lane & HALF) | ((lane - by) & (HALF - 1)) for by in (-2, -1, 1, 2)}
         z = lax.broadcasted_iota(jnp.int32, (Z, L), 0)
         self.z0, self.z1 = z == 0, z == 1
         self.z_last, self.z_before = z == Z - 1, z == Z - 2
 
     def kx(self, row, by):
-        mask, wrapped = {
-            -1: (self.kx_last, HALF - 1),
-            -2: (self.kx_pair, HALF - 2),
-            1: (self.kx_first, HALF + 1),
-            2: (self.kx_second, HALF + 2),
-        }[by]
-        return jnp.where(mask, pltpu.roll(row, wrapped, 1), pltpu.roll(row, by % L, 1))
+        return jnp.take_along_axis(row, self.moved[by], axis=1)
 
     def kz_next(self, row, after):
         return jnp.where(self.z_last, after, pltpu.roll(row, Z - 1, 0))
@@ -116,18 +108,14 @@
 
 def along_kx(sh, u, digit):
     low, centre, high, far = terms(digit, u - sh.kx(u, -1))
-    return sh.kx(low, -1) + centre + sh.kx(high, 1) + sh.kx(far, 2)
+    return sh.kx(low, -1) + centre + sh.kx(high + sh.kx(far, 1), 1)
 
 
 def along_kz(sh, u, digit, above, t_above, digit_b, below, s_below):
     low, centre, high, far = terms(digit, u - sh.kz_next(u, above))
     edge = below - u[0:1]
-    return (
-        sh.kz_next(low, t_above)
-        + centre
-        + sh.kz_prev(high, c_high(digit_b) * edge)
-        + sh.kz_prev2(far, c_far(digit_b) * edge, s_below)
-    )
+    far = sh.kz_prev(far, c_far(digit_b) * edge)
+    return sh.kz_next(low, t_above) + centre + sh.kz_prev(high + far, c_high(digit_b) * edge + s_below)
 
 
 def along_ky(sh, rows, digit_rows, above, t_above, digit_b, below, s_below):
@@ -197,7 +185,9 @@
             left, right, (((1,), (1,)), ((), ())), preferred_element_type=F32
         )
 
-    both = lax.fori_loop(0, R, body, jnp.zeros((2 * X, SHELLS), F32))
+    both = jnp.zeros((2 * X, SHELLS), F32)
+    for r in range(R):
+        both = body(r, both)
     return both[:X] + both[X:]
 
 
@@ -208,10 +198,10 @@
 
 
 def edges_kernel(
-    u_hbm, code_hbm, start_hbm, vel_hbm, pos_up, pos_down, ky_up, ky_down, kz_up, kz_down,
-    u_ref, code_ref, start_ref, vel_ref, arrived,
+    u_hbm, code_hbm, start_hbm, vel_hbm, field_hbm, pos_up, pos_down, ky_up, ky_down, kz_up, kz_down,
+    u_ref, code_ref, start_ref, vel_ref, field_ref, arrived,
 ):
-    pairs = ((u_hbm, u_ref), (code_hbm, code_ref), (vel_hbm, vel_ref), (start_hbm, start_ref))
+    pairs = ((u_hbm, u_ref), (code_hbm, code_ref), (vel_hbm, vel_ref), (start_hbm, start_ref), (field_hbm, field_ref))
     copies = [pltpu.make_async_copy(a, b, arrived.at[n]) for n, (a, b) in enumerate(pairs)]
     for copy in copies:
         copy.start()
@@ -261,6 +251,7 @@
         kz_down[1, x] = c_low(d_first) * (first - second)
         kz_down[2, x] = plane(start_ref, x, 0)
         kz_down[3, x] = plane(start_ref, x, 1)
+    copies[4].wait()
 
 
 def first_sums_kernel(
@@ -532,14 +523,14 @@
     plane, ky_plane, kz_plane = (R, Z, L), (X, Z, L), (X, R, L)
     w_scratch = [pltpu.VMEM((R, 2 * X * Z, L), F32)]
     sums_shape = ((members, X, L), None)
-    up, down, ky_up, ky_down, kz_up, kz_down, u_v, code_v, start_v, vel_v = call(
+    up, down, ky_up, ky_down, kz_up, kz_down, u_v, code_v, start_v, vel_v, field_v = call(
         edges_kernel,
         [((3,) + plane, None), ((2,) + plane, None), ((3,) + ky_plane, None), ((2,) + ky_plane, None),
          ((5,) + kz_plane, None), ((4,) + kz_plane, None), (cotangent.shape, None), (cotangent.shape, jnp.int32),
-         (cotangent.shape, None), (velocity.shape, None)],
-        [cotangent, face_codes, start_state, velocity],
+         (cotangent.shape, None), (velocity.shape, None), (field_strength.shape, None)],
+        [cotangent, face_codes, start_state, velocity, field_strength],
         in_hbm=True,
-        scratch=[pltpu.SemaphoreType.DMA((4,))],
+        scratch=[pltpu.SemaphoreType.DMA((5,))],
         ops=4_000_000,
     )
     up, down = shift_both(up, down, "pos", False)
@@ -549,7 +540,7 @@
         first_sums_kernel,
         [(FULL, None), (FULL, None), ((3,) + plane, None), (plane, jnp.int32), ((3, X, R, L), None),
          (FULL, None), (FULL, None), sums_shape],
-        [field_strength, u_v, code_v, vel_v, shell_index, shell_out, shell_in, section_state, start_v],
+        [field_v, u_v, code_v, vel_v, shell_index, shell_out, shell_in, section_state, start_v],
         scratch=w_scratch,
         ops=8_000_000,
     )

time: 98.8 us -> 94.9 us (0.961)
  Pallas kernels: 15.8 us -> 12.5 us
    pallas_call x8, Pallas kernels: 15.8 us -> 12.5 us  [call(): pl.pallas_call(kernel, out_shape=shapes, in_specs=[given] * len(args), ou...]
  transfers between devices with their start and end apart: 14 -> 14, of which waited for: 4 -> 4; matrix products, arithmetic and copies ran while one was open for 0% -> 0% of each run, Pallas kernels for 7% -> 6%
where the time goes in v4:
time: 94.9 us; the launch traced here: 94.4 us
  starting transfers between devices  56.6 us (60%)
  waiting for transfers between devices  24.4 us (26%)
  Pallas kernels  12.5 us (13%)
    ppermute x12, starting transfers between devices, shift(): return lax.ppermute(array, axis, pairs)  39.3 us
    ppermute x12, waiting for transfers between devices, shift(): return lax.ppermute(array, axis, pairs)  24.4 us
    all_to_all x2, starting transfers between devices, exchange(): return lax.all_to_all(copies, ('ky', 'kz'), 0, 0)  17.3 us
    pallas_call x8, Pallas kernels, call(): pl.pallas_call(kernel, out_shape=shapes, in_specs=[given] * len(args), ou...  12.5 us
  transfers between devices with their start and end apart: 14, of which 4 were waited for; matrix products, arithmetic and copies ran while one was open for 0% of the time, Pallas kernels for 6%

profile of v4, /device:TPU:23, one launch (start us, length us, event | category | flops | bytes accessed | tf_op | source)
XLA Modules:
  0.0 94.4 jit_solution(7740443055421613023)
XLA Ops:
  0.7 2.4 %shard_map.104 = (f32[3,8,16,128]{3,2,1,0:T(8,128)S(1)}, f32[2,8,16,128]{3,2,1,0:T(8,128)S(1)}, f32[3,4,16,128]{3,2,1,0:T(8,128)S(1)}, f32[2,4,16,128]{3,2,1,0:T...) custom-call(f32[4,16,16,64]{3,2,1,0:T(8,128)} %u_hbm.1, ...), custom_call_target="tpu_custom_call" | custom-call | flops 4000000 | bytes 2343008 | tf_op jit(solution)/shard_map/pallas_call | solution.py:483
  3.2 1.4 %shard_map.105 = (f32[4,8,16,128]{3,2,1,0:T(8,128)S(1)}, f32[4,8,16,128]{3,2,1,0:T(8,128)S(1)}, f32[3,8,16,128]{3,2,1,0:T(8,128)S(1)}, s32[8,16,128]{2,1,0:T(8,1...) custom-call(f32[3,4]{1,0:T(4,128)S(1)} %get-tuple-element.30.field, ...), custom_call_target="tpu_custom_call" | custom-call | flops 8000000 | bytes 2736176 | tf_op jit(solution)/shard_map/pallas_call | solution.py:483
  4.6 9.3 %all-to-all-start = ((f32[32,4,128]{2,1,0:T(4,128)}), f32[32,4,128]{2,1,0:T(4,128)S(1)}, u32[]{:S(2)}, u32[]{:S(2)}) async-start(f32[32,4,128]{2,1,0:T(4,128)} %get-tuple-element.49), calls=%async_computation | async-start | bytes 131072 | tf_op jit(solution)/shard_map/all_to_all | solution.py:508
  13.9 8.8 %collective-permute-start.4 = (f32[3,8,16,128]{3,2,1,0:T(8,128)S(1)}, f32[3,8,16,128]{3,2,1,0:T(8,128)S(1)}, u32[]{:S(2)}, u32[]{:S(2)}) collective-permute-start(f32[3,8,16,128]{3,2,1,0:T(8,128)S(1)} %get-tuple-element.47), channel_id=1, source_target_pairs={{0,32},{32,64},{64,96},{96,128},{128,160},{160,192},{192,224},{224... | collective-permute-start | bytes 589832 | tf_op jit(solution)/shard_map/ppermute | solution.py:498
  22.7 5.0 %collective-permute-start.1 = (f32[2,4,16,128]{3,2,1,0:T(8,128)}, f32[2,4,16,128]{3,2,1,0:T(8,128)S(1)}, u32[]{:S(2)}, u32[]{:S(2)}) collective-permute-start(f32[2,4,16,128]{3,2,1,0:T(8,128)} %get-tuple-element.42), channel_id=1, source_target_pairs={{0,24},{8,0},{16,8},{24,16},{1,25},{9,1},{17,9},{25,17},{2,26},{10... | collective-permute-start | bytes 196616 | tf_op jit(solution)/shard_map/ppermute | solution.py:498
  27.7 2.7 %collective-permute-start.5 = (f32[2,8,16,128]{3,2,1,0:T(8,128)S(1)}, f32[2,8,16,128]{3,2,1,0:T(8,128)S(1)}, u32[]{:S(2)}, u32[]{:S(2)}) collective-permute-start(f32[2,8,16,128]{3,2,1,0:T(8,128)S(1)} %get-tuple-element.48), channel_id=1, source_target_pairs={{32,0},{64,32},{96,64},{128,96},{160,128},{192,160},{224,192},{256... | collective-permute-start | bytes 393224 | tf_op jit(solution)/shard_map/ppermute | solution.py:498
  30.4 1.9 %collective-permute-start = (f32[3,4,16,128]{3,2,1,0:T(8,128)S(1)}, f32[3,4,16,128]{3,2,1,0:T(8,128)S(1)}, u32[]{:S(2)}, u32[]{:S(2)}) collective-permute-start(f32[3,4,16,128]{3,2,1,0:T(8,128)S(1)} %get-tuple-element.41), channel_id=1, source_target_pairs={{0,8},{8,16},{16,24},{24,0},{1,9},{9,17},{17,25},{25,1},{2,10},{10... | collective-permute-start | bytes 294920 | tf_op jit(solution)/shard_map/ppermute | solution.py:498
  32.4 1.1 %collective-permute-start.2 = (f32[5,4,8,128]{3,2,1,0:T(8,128)S(1)}, f32[5,4,8,128]{3,2,1,0:T(8,128)S(1)}, u32[]{:S(2)}, u32[]{:S(2)}) collective-permute-start(f32[5,4,8,128]{3,2,1,0:T(8,128)S(1)} %get-tuple-element.43), channel_id=1, source_target_pairs={{0,1},{1,2},{2,3},{3,4},{4,5},{5,6},{6,7},{7,0},{8,9},{9,10},{10,1... | collective-permute-start | bytes 245768 | tf_op jit(solution)/shard_map/ppermute | solution.py:498
  33.5 8.8 %collective-permute-done.1.ky_down = f32[2,4,16,128]{3,2,1,0:T(8,128)S(1)} collective-permute-done((f32[2,4,16,128]{3,2,1,0:T(8,128)}, f32[2,4,16,128]{3,2,1,0:T(8,128)S(1)}, u32[]{:S(2)}, u32[]{:S(2)}) %collective-permute-start.1) | collective-permute-done | bytes 65568 | tf_op jit(solution)/shard_map/ppermute | solution.py:498
  42.2 0.6 collective-permute-start.3
  42.8 4.3 %collective-permute-done.3.kz_down = f32[4,4,8,128]{3,2,1,0:T(8,128)S(1)} collective-permute-done((f32[4,4,8,128]{3,2,1,0:T(8,128)S(1)}, f32[4,4,8,128]{3,2,1,0:T(8,128)S(1)}, u32[]{:S(2)}, u32[]{:S(2)}) %collective-permute-start.3) | collective-permute-done | bytes 65568 | tf_op jit(solution)/shard_map/ppermute | solution.py:498
  47.1 0.0 collective-permute-done.2.kz_up.first_kz
  47.1 0.0 collective-permute-done.ky_up.first_up
  47.1 3.6 %shard_map.106 = (f32[4,8,16,128]{3,2,1,0:T(8,128)S(1)}, f32[3,4,9,16,128]{4,3,2,1,0:T(8,128)S(1)}) custom-call(f32[3,4,8,128]{3,2,1,0:T(8,128)S(1)} %get-tuple-element.35.field, f32[4,8,16,128]{3,2,1,0:T(8,128)S(1)} %get-tuple-element.36.u_p, f32[4,8,16,128]{3,2,1,0:T(8,128)S(1)} %get-tuple-element.37.code_p, ...), custom_call_target="tpu_custom_call" | custom-call | flops 16000000 | bytes 2752512 | tf_op jit(solution)/shard_map/pallas_call | solution.py:483
  50.7 0.0 collective-permute-done.5.got_down
  50.7 0.0 all-to-all-done.got_sums
  50.7 0.8 shard_map.107
  51.5 1.4 %shard_map.110 = f32[32,4,128]{2,1,0:T(4,128)} custom-call(f32[4,8,16,128]{3,2,1,0:T(8,128)S(1)} %get-tuple-element.50.section, f32[3,8,16,128]{3,2,1,0:T(8,128)S(1)} %get-tuple-element.38.fields_p, s32[8,16,128]{2,1,0:T(8,128)S(1)} %get-tuple-element.46.shell_p, f32[3,4,9,16,128]{4,3,2,1,0:T(8,128)S(1)} %get-tuple-element.57.slopes), custom_call_target="tpu_custom_call" | custom-call | flops 4000000 | bytes 1474560 | tf_op jit(solution)/shard_map/pallas_call | solution.py:483
  52.9 8.0 %all-to-all-start.1 = ((f32[32,4,128]{2,1,0:T(4,128)}), f32[32,4,128]{2,1,0:T(4,128)S(1)}, u32[]{:S(2)}, u32[]{:S(2)}) async-start(f32[32,4,128]{2,1,0:T(4,128)} %shard_map.110), calls=%async_computation.1 | async-start | bytes 131072 | tf_op jit(solution)/shard_map/all_to_all | solution.py:508
  60.9 5.9 %collective-permute-start.10 = (f32[2,8,16,128]{3,2,1,0:T(8,128)S(1)}, f32[2,8,16,128]{3,2,1,0:T(8,128)S(1)}, u32[]{:S(2)}, u32[]{:S(2)}) collective-permute-start(f32[2,8,16,128]{3,2,1,0:T(8,128)S(1)} %get-tuple-element.55), channel_id=1, source_target_pairs={{0,32},{32,64},{64,96},{96,128},{128,160},{160,192},{192,224},{224... | collective-permute-start | bytes 393224 | tf_op jit(solution)/shard_map/ppermute | solution.py:498
  66.8 4.2 %collective-permute-start.11 = (f32[2,8,16,128]{3,2,1,0:T(8,128)S(1)}, f32[2,8,16,128]{3,2,1,0:T(8,128)S(1)}, u32[]{:S(2)}, u32[]{:S(2)}) collective-permute-start(f32[2,8,16,128]{3,2,1,0:T(8,128)S(1)} %get-tuple-element.56), channel_id=1, source_target_pairs={{32,0},{64,32},{96,64},{128,96},{160,128},{192,160},{224,192},{256... | collective-permute-start | bytes 393224 | tf_op jit(solution)/shard_map/ppermute | solution.py:498
  71.0 0.3 shard_map.108
  71.3 3.1 %collective-permute-start.6 = (f32[4,16,128]{2,1,0:T(8,128)S(1)}, f32[4,16,128]{2,1,0:T(8,128)S(1)}, u32[]{:S(2)}, u32[]{:S(2)}) collective-permute-start(f32[4,16,128]{2,1,0:T(8,128)S(1)} %get-tuple-element.51), channel_id=1, source_target_pairs={{0,8},{8,16},{16,24},{24,0},{1,9},{9,17},{17,25},{25,1},{2,10},{10... | collective-permute-start | bytes 98312 | tf_op jit(solution)/shard_map/ppermute | solution.py:498
  74.4 4.0 %collective-permute-start.7 = (f32[4,16,128]{2,1,0:T(8,128)S(1)}, f32[4,16,128]{2,1,0:T(8,128)S(1)}, u32[]{:S(2)}, u32[]{:S(2)}) collective-permute-start(f32[4,16,128]{2,1,0:T(8,128)S(1)} %get-tuple-element.52), channel_id=1, source_target_pairs={{0,24},{8,0},{16,8},{24,16},{1,25},{9,1},{17,9},{25,17},{2,26},{10... | collective-permute-start | bytes 98312 | tf_op jit(solution)/shard_map/ppermute | solution.py:498
  78.4 1.4 %collective-permute-start.8 = (f32[2,4,8,128]{3,2,1,0:T(8,128)S(1)}, f32[2,4,8,128]{3,2,1,0:T(8,128)S(1)}, u32[]{:S(2)}, u32[]{:S(2)}) collective-permute-start(f32[2,4,8,128]{3,2,1,0:T(8,128)S(1)} %get-tuple-element.53), channel_id=1, source_target_pairs={{0,1},{1,2},{2,3},{3,4},{4,5},{5,6},{6,7},{7,0},{8,9},{9,10},{10,1... | collective-permute-start | bytes 98312 | tf_op jit(solution)/shard_map/ppermute | solution.py:498
  79.7 7.5 %collective-permute-done.6.ky_up = f32[4,16,128]{2,1,0:T(8,128)S(1)} collective-permute-done((f32[4,16,128]{2,1,0:T(8,128)S(1)}, f32[4,16,128]{2,1,0:T(8,128)S(1)}, u32[]{:S(2)}, u32[]{:S(2)}) %collective-permute-start.6) | collective-permute-done | bytes 32800 | tf_op jit(solution)/shard_map/ppermute | solution.py:498
  87.2 0.7 collective-permute-start.9
  87.9 0.0 collective-permute-done.8.kz_up
  87.9 3.9 %collective-permute-done.9.kz_down = f32[2,4,8,128]{3,2,1,0:T(8,128)S(1)} collective-permute-done((f32[2,4,8,128]{3,2,1,0:T(8,128)S(1)}, f32[2,4,8,128]{3,2,1,0:T(8,128)S(1)}, u32[]{:S(2)}, u32[]{:S(2)}) %collective-permute-start.9) | collective-permute-done | bytes 32800 | tf_op jit(solution)/shard_map/ppermute | solution.py:498
  91.7 1.4 %shard_map.109.partial = f32[4,8,16,128]{3,2,1,0:T(8,128)S(1)} custom-call(f32[3,4,8,128]{3,2,1,0:T(8,128)S(1)} %get-tuple-element.35.field, f32[4,8,16,128]{3,2,1,0:T(8,128)S(1)} %get-tuple-element.50.section, f32[4,8,16,128]{3,2,1,0:T(8,128)S(1)} %get-tuple-element.36.u_p, f32[4,8,16,128]{3,2,1,0:T(8,128)S(1)} %get-tuple-element.37.code_p, ...), custom_call_target="tpu_custom_call" | custom-call | flops 8000000 | bytes 1605632 | tf_op jit(solution)/shard_map/pallas_call | solution.py:483
  93.2 0.0 collective-permute-done.11.got_down
  93.2 1.2 %shard_map.111 = (f32[4,16,16,64]{3,2,1,0:T(8,128)}, f32[3,4]{1,0:T(4,128)}) custom-call(f32[4,8,16,128]{3,2,1,0:T(8,128)S(1)} %shard_map.109.partial, f32[4,8,16,128]{3,2,1,0:T(8,128)S(1)} %get-tuple-element.50.section, f32[4,8,16,128]{3,2,1,0:T(8,128)S(1)} %get-tuple-element.37.code_p, f32[3,8,16,128]{3,2,1,0:T(8,128)S(1)} %get-tuple-element.38.fields_p, ...), custom_call_target="tpu_custom_call" | custom-call | flops 3000000 | bytes 1835056 | tf_op jit(solution)/shard_map/pallas_call | solution.py:483
  (12 shorter events, 0.0 us)
Async XLA Ops:
  0.6 2.5 %copy-start.3 = (f32[16,16,64]{2,1,0:T(8,128)S(1)}, f32[16,16,64]{2,1,0:T(8,128)}, u32[]{:S(2)}) copy-start(f32[16,16,64]{2,1,0:T(8,128)} %in_ref.1) | copy-start | bytes 196612
  0.6 2.5 %copy-start.2 = (f32[16,16,64]{2,1,0:T(8,128)S(1)}, f32[16,16,64]{2,1,0:T(8,128)}, u32[]{:S(2)}) copy-start(f32[16,16,64]{2,1,0:T(8,128)} %out_ref.1) | copy-start | bytes 196612
  0.7 2.5 %copy-start.1 = (s32[16,16,64]{2,1,0:T(8,128)S(1)}, s32[16,16,64]{2,1,0:T(8,128)}, u32[]{:S(2)}) copy-start(s32[16,16,64]{2,1,0:T(8,128)} %shell_ref.1) | copy-start | bytes 196612
  0.7 2.5 %copy-start = (f32[4,16,16,64]{3,2,1,0:T(8,128)S(1)}, f32[4,16,16,64]{3,2,1,0:T(8,128)}, u32[]{:S(2)}) copy-start(f32[4,16,16,64]{3,2,1,0:T(8,128)} %section_ref.1) | copy-start | bytes 786436
  4.6 46.1 %all-to-all-start = ((f32[32,4,128]{2,1,0:T(4,128)}), f32[32,4,128]{2,1,0:T(4,128)S(1)}, u32[]{:S(2)}, u32[]{:S(2)}) async-start(f32[32,4,128]{2,1,0:T(4,128)} %get-tuple-element.49), calls=%async_computation | async-start | bytes 131072 | tf_op jit(solution)/shard_map/all_to_all | solution.py:508
  13.9 36.8 %collective-permute-start.4 = (f32[3,8,16,128]{3,2,1,0:T(8,128)S(1)}, f32[3,8,16,128]{3,2,1,0:T(8,128)S(1)}, u32[]{:S(2)}, u32[]{:S(2)}) collective-permute-start(f32[3,8,16,128]{3,2,1,0:T(8,128)S(1)} %get-tuple-element.47), channel_id=1, source_target_pairs={{0,32},{32,64},{64,96},{96,128},{128,160},{160,192},{192,224},{224... | collective-permute-start | bytes 589832 | tf_op jit(solution)/shard_map/ppermute | solution.py:498
  22.7 19.5 %collective-permute-start.1 = (f32[2,4,16,128]{3,2,1,0:T(8,128)}, f32[2,4,16,128]{3,2,1,0:T(8,128)S(1)}, u32[]{:S(2)}, u32[]{:S(2)}) collective-permute-start(f32[2,4,16,128]{3,2,1,0:T(8,128)} %get-tuple-element.42), channel_id=1, source_target_pairs={{0,24},{8,0},{16,8},{24,16},{1,25},{9,1},{17,9},{25,17},{2,26},{10... | collective-permute-start | bytes 196616 | tf_op jit(solution)/shard_map/ppermute | solution.py:498
  27.7 23.0 %collective-permute-start.5 = (f32[2,8,16,128]{3,2,1,0:T(8,128)S(1)}, f32[2,8,16,128]{3,2,1,0:T(8,128)S(1)}, u32[]{:S(2)}, u32[]{:S(2)}) collective-permute-start(f32[2,8,16,128]{3,2,1,0:T(8,128)S(1)} %get-tuple-element.48), channel_id=1, source_target_pairs={{32,0},{64,32},{96,64},{128,96},{160,128},{192,160},{224,192},{256... | collective-permute-start | bytes 393224 | tf_op jit(solution)/shard_map/ppermute | solution.py:498
  30.4 16.7 %collective-permute-start = (f32[3,4,16,128]{3,2,1,0:T(8,128)S(1)}, f32[3,4,16,128]{3,2,1,0:T(8,128)S(1)}, u32[]{:S(2)}, u32[]{:S(2)}) collective-permute-start(f32[3,4,16,128]{3,2,1,0:T(8,128)S(1)} %get-tuple-element.41), channel_id=1, source_target_pairs={{0,8},{8,16},{16,24},{24,0},{1,9},{9,17},{17,25},{25,1},{2,10},{10... | collective-permute-start | bytes 294920 | tf_op jit(solution)/shard_map/ppermute | solution.py:498
  32.4 14.7 %collective-permute-start.2 = (f32[5,4,8,128]{3,2,1,0:T(8,128)S(1)}, f32[5,4,8,128]{3,2,1,0:T(8,128)S(1)}, u32[]{:S(2)}, u32[]{:S(2)}) collective-permute-start(f32[5,4,8,128]{3,2,1,0:T(8,128)S(1)} %get-tuple-element.43), channel_id=1, source_target_pairs={{0,1},{1,2},{2,3},{3,4},{4,5},{5,6},{6,7},{7,0},{8,9},{9,10},{10,1... | collective-permute-start | bytes 245768 | tf_op jit(solution)/shard_map/ppermute | solution.py:498
  42.2 4.9 %collective-permute-start.3 = (f32[4,4,8,128]{3,2,1,0:T(8,128)S(1)}, f32[4,4,8,128]{3,2,1,0:T(8,128)S(1)}, u32[]{:S(2)}, u32[]{:S(2)}) collective-permute-start(f32[4,4,8,128]{3,2,1,0:T(8,128)S(1)} %get-tuple-element.44), channel_id=1, source_target_pairs={{0,7},{1,0},{2,1},{3,2},{4,3},{5,4},{6,5},{7,6},{8,15},{9,8},{10,9... | collective-permute-start | bytes 196616 | tf_op jit(solution)/shard_map/ppermute | solution.py:498
  52.9 40.3 %all-to-all-start.1 = ((f32[32,4,128]{2,1,0:T(4,128)}), f32[32,4,128]{2,1,0:T(4,128)S(1)}, u32[]{:S(2)}, u32[]{:S(2)}) async-start(f32[32,4,128]{2,1,0:T(4,128)} %shard_map.110), calls=%async_computation.1 | async-start | bytes 131072 | tf_op jit(solution)/shard_map/all_to_all | solution.py:508
  60.9 32.3 %collective-permute-start.10 = (f32[2,8,16,128]{3,2,1,0:T(8,128)S(1)}, f32[2,8,16,128]{3,2,1,0:T(8,128)S(1)}, u32[]{:S(2)}, u32[]{:S(2)}) collective-permute-start(f32[2,8,16,128]{3,2,1,0:T(8,128)S(1)} %get-tuple-element.55), channel_id=1, source_target_pairs={{0,32},{32,64},{64,96},{96,128},{128,160},{160,192},{192,224},{224... | collective-permute-start | bytes 393224 | tf_op jit(solution)/shard_map/ppermute | solution.py:498
  66.8 26.4 %collective-permute-start.11 = (f32[2,8,16,128]{3,2,1,0:T(8,128)S(1)}, f32[2,8,16,128]{3,2,1,0:T(8,128)S(1)}, u32[]{:S(2)}, u32[]{:S(2)}) collective-permute-start(f32[2,8,16,128]{3,2,1,0:T(8,128)S(1)} %get-tuple-element.56), channel_id=1, source_target_pairs={{32,0},{64,32},{96,64},{128,96},{160,128},{192,160},{224,192},{256... | collective-permute-start | bytes 393224 | tf_op jit(solution)/shard_map/ppermute | solution.py:498
  71.3 15.9 %collective-permute-start.6 = (f32[4,16,128]{2,1,0:T(8,128)S(1)}, f32[4,16,128]{2,1,0:T(8,128)S(1)}, u32[]{:S(2)}, u32[]{:S(2)}) collective-permute-start(f32[4,16,128]{2,1,0:T(8,128)S(1)} %get-tuple-element.51), channel_id=1, source_target_pairs={{0,8},{8,16},{16,24},{24,0},{1,9},{9,17},{17,25},{25,1},{2,10},{10... | collective-permute-start | bytes 98312 | tf_op jit(solution)/shard_map/ppermute | solution.py:498
  74.4 13.5 %collective-permute-start.7 = (f32[4,16,128]{2,1,0:T(8,128)S(1)}, f32[4,16,128]{2,1,0:T(8,128)S(1)}, u32[]{:S(2)}, u32[]{:S(2)}) collective-permute-start(f32[4,16,128]{2,1,0:T(8,128)S(1)} %get-tuple-element.52), channel_id=1, source_target_pairs={{0,24},{8,0},{16,8},{24,16},{1,25},{9,1},{17,9},{25,17},{2,26},{10... | collective-permute-start | bytes 98312 | tf_op jit(solution)/shard_map/ppermute | solution.py:498
  78.4 9.5 %collective-permute-start.8 = (f32[2,4,8,128]{3,2,1,0:T(8,128)S(1)}, f32[2,4,8,128]{3,2,1,0:T(8,128)S(1)}, u32[]{:S(2)}, u32[]{:S(2)}) collective-permute-start(f32[2,4,8,128]{3,2,1,0:T(8,128)S(1)} %get-tuple-element.53), channel_id=1, source_target_pairs={{0,1},{1,2},{2,3},{3,4},{4,5},{5,6},{6,7},{7,0},{8,9},{9,10},{10,1... | collective-permute-start | bytes 98312 | tf_op jit(solution)/shard_map/ppermute | solution.py:498
  87.2 4.6 %collective-permute-start.9 = (f32[2,4,8,128]{3,2,1,0:T(8,128)S(1)}, f32[2,4,8,128]{3,2,1,0:T(8,128)S(1)}, u32[]{:S(2)}, u32[]{:S(2)}) collective-permute-start(f32[2,4,8,128]{3,2,1,0:T(8,128)S(1)} %get-tuple-element.54), channel_id=1, source_target_pairs={{0,7},{1,0},{2,1},{3,2},{4,3},{5,4},{6,5},{7,6},{8,15},{9,8},{10,9... | collective-permute-start | bytes 98312 | tf_op jit(solution)/shard_map/ppermute | solution.py:498
